TPU v7x, 512 devices: a whole 4x8x8 slice. The times are simulated.
512 devices in a mesh: dp: 32 (over y_lo, z, core), expert: 16 (over y_hi, x).
Axes of the slice: x: 4, y: 8 (y_hi: 4, y_lo: 2; y = y_hi * 2 + y_lo), z: 8, core: 2. Of those that a mesh axis runs over, the one named last changes fastest.
Arguments:
- tokens: bfloat16 [65536, 2048], P(('dp', 'expert')), may hold values from -6 to 6
- routes: int32 [65536, 2], P(('dp', 'expert')), may hold values from 0 to 15, all different within a row; in each aligned block of 128 rows (0 to 127, 128 to 255, ...) at most 32 rows name the same one
- gate_values: float32 [65536, 2], P(('dp', 'expert')), may hold values from 0.1 to 1
- gate_weight: bfloat16 [16, 2048, 768], P('expert', 'dp'), may hold values from -0.125 to 0.125
- up_weight: bfloat16 [16, 2048, 768], P('expert', 'dp'), may hold values from -0.125 to 0.125
- down_weight: bfloat16 [16, 768, 2048], P('expert', None, 'dp'), may hold values from -0.21875 to 0.21875
Outputs:
- mixture: bfloat16 [65536, 2048], P(('dp', 'expert'))
Inputs may be any that keep to these rules, and one draw needn't show every extreme that they name: `routes`: in the rows of one device no expert is named by more than 32 rows, and in every draw some device's rows name some expert exactly 32 times.
All inputs are finite; a program needn't handle non-finite values.
Results may differ from a plain program's by a relative error of at most 0.0057.
Values may be sent and summed in bfloat16 or wider, within the bound.
No kernel may reach another device: no remote copies, remote signals or barrier semaphores. Data moves between devices by JAX's collectives and lax.ppermute only.
A program may use at most 64 MiB of HBM per device.

v0:
```python
import jax
import jax.numpy as jnp
from jax import lax
from jax.sharding import PartitionSpec as P

tile_height = 128


def pack_rows(blocks, counts):
    sources, capacity, features = blocks.shape
    slot_total = sources * capacity
    padded_total = -(-slot_total // tile_height) * tile_height
    block_ends = jnp.cumsum(counts)
    starts = block_ends - counts
    live_rows = block_ends[-1]
    packed_index = jnp.arange(padded_total, dtype=jnp.int32)
    source_of = jnp.minimum(
        jnp.sum((packed_index[:, None] >= block_ends[None, :]).astype(jnp.int32), axis=1),
        sources - 1,
    )
    within = packed_index - starts[source_of]
    gather_index = jnp.clip(source_of * capacity + within, 0, slot_total - 1)
    packed = blocks.reshape(slot_total, features)[gather_index]
    tile_count = (live_rows + tile_height - 1) // tile_height
    return (packed, starts, tile_count)


def hidden_tiles(packed, tile_count, gate_part, up_part):
    width = gate_part.shape[1]

    def hidden_one_tile(tile_number, hidden):
        offset = tile_number * tile_height
        selected = lax.dynamic_slice_in_dim(packed, offset, tile_height, 0)
        gated = jnp.dot(selected, gate_part, preferred_element_type=jnp.float32)
        upward = jnp.dot(selected, up_part, preferred_element_type=jnp.float32)
        values = (jax.nn.silu(gated) * upward).astype(jnp.bfloat16)
        return lax.dynamic_update_slice_in_dim(hidden, values, offset, 0)

    return lax.fori_loop(
        0, tile_count, hidden_one_tile, jnp.zeros((packed.shape[0], width), jnp.bfloat16)
    )


def down_tiles(hidden, tile_count, down_part):

    def down_one_tile(tile_number, results):
        offset = tile_number * tile_height
        selected = lax.dynamic_slice_in_dim(hidden, offset, tile_height, 0)
        values = jnp.dot(selected, down_part, preferred_element_type=jnp.float32).astype(
            jnp.bfloat16
        )
        return lax.dynamic_update_slice_in_dim(results, values, offset, 0)

    return lax.fori_loop(
        0, tile_count, down_one_tile, jnp.zeros((hidden.shape[0], down_part.shape[1]), jnp.bfloat16)
    )


def unpack_rows(results, starts, counts, capacity):
    sources = counts.shape[0]
    padded_total = results.shape[0]
    slot_index = jnp.arange(capacity, dtype=jnp.int32)
    position = jnp.minimum(starts[:, None] + slot_index[None, :], padded_total - 1)
    unpacked = results[position.reshape(-1)].reshape(sources, capacity, results.shape[1])
    filled = slot_index[None, :] < counts[:, None]
    return jnp.where(filled[:, :, None], unpacked, jnp.zeros_like(unpacked))


def per_device(tokens, routes, gate_values, gate_weight, up_weight, down_weight):
    groups = lax.axis_size("expert")
    token_count = tokens.shape[0]
    features = tokens.shape[1]
    top_count = routes.shape[1]
    capacity = 2 * token_count * top_count // groups
    flat_routes = routes.reshape(-1)
    member = (flat_routes[:, None] == jnp.arange(groups, dtype=jnp.int32)[None, :]).astype(
        jnp.int32
    )
    running = jnp.cumsum(member, axis=0)
    in_block = jnp.sum(member * (running - 1), axis=1)
    counts = jnp.sum(member, axis=0)
    destination = flat_routes * capacity + in_block
    source_rows = jnp.arange(flat_routes.shape[0], dtype=jnp.int32) // top_count
    owner_rows = (
        jnp.full((groups * capacity,), token_count, jnp.int32).at[destination].set(source_rows)
    )
    picked = tokens[jnp.minimum(owner_rows, token_count - 1)]
    outgoing = jnp.where((owner_rows < token_count)[:, None], picked, jnp.zeros_like(picked))
    outgoing = outgoing.reshape(groups, capacity, features)
    arrived, arrived_counts = (
        lax.all_to_all(outgoing, "expert", split_axis=0, concat_axis=0, tiled=True),
        lax.all_to_all(counts, "expert", split_axis=0, concat_axis=0, tiled=True),
    )
    packed, starts, tile_count = pack_rows(arrived, arrived_counts)
    gathered = (
        lax.all_gather(gate_weight[0], "dp", axis=0, tiled=True),
        lax.all_gather(up_weight[0], "dp", axis=0, tiled=True),
        lax.all_gather(down_weight[0], "dp", axis=1, tiled=True),
    )
    hidden = hidden_tiles(packed, tile_count, gathered[0], gathered[1])
    results = down_tiles(hidden, tile_count, gathered[2])
    produced = unpack_rows(results, starts, arrived_counts, capacity)
    returned = lax.all_to_all(produced, "expert", split_axis=0, concat_axis=0, tiled=True)
    slot_results = returned.reshape(groups * capacity, features)[destination].reshape(
        token_count, top_count, features
    )
    mixture = jnp.zeros((token_count, features), jnp.float32)
    for column in range(top_count):
        mixture = mixture + gate_values[:, column : column + 1] * slot_results[:, column, :].astype(
            jnp.float32
        )
    return mixture.astype(jnp.bfloat16)


def solution(mesh):
    placed = (
        P(("dp", "expert"), None),
        P(("dp", "expert"), None),
        P(("dp", "expert"), None),
        P("expert", "dp", None),
        P("expert", "dp", None),
        P("expert", None, "dp"),
    )
    return jax.shard_map(
        per_device, mesh=mesh, in_specs=placed, out_specs=P(("dp", "expert"), None), check_vma=False
    )
```

profile of v0, /device:TPU:1, one launch (start us, length us, event | category | flops | bytes accessed | tf_op | source)
XLA Modules:
  0.0 329.2 jit_solution(456294467491526725)
XLA Ops:
  10.7 10.2 %all-to-all-start = ((s32[16,1,1]{2,1,0:T(1,128)}), s32[16,1,1]{2,1,0:T(1,128)S(1)}, u32[]{:S(2)}, u32[]{:S(2)}) async-start(s32[16,1,1]{2,1,0:T(1,128)} %copy.38), calls=%async_computation | async-start | bytes 16384 | tf_op jit(solution)/shard_map/all_to_all | solution.py:92
  23.4 2.5 gather_fusion
  27.4 2.3 all-to-all-done
  29.7 6.8 %all-to-all-start.1 = ((bf16[16,32,2048]{2,1,0:T(8,128)(2,1)}), bf16[16,32,2048]{2,1,0:T(8,128)(2,1)S(1)}, u32[]{:S(2)}, u32[]{:S(2)}) async-start(bf16[16,32,2048]{2,1,0:T(8,128)(2,1)} %broadcast_select_fusion), calls=%async_computation.1 | async-start | bytes 4194304 | tf_op jit(solution)/shard_map/all_to_all | solution.py:91
  39.9 4.5 %compare_select_fusion.3 = (s32[512,1]{0,1:T(1,128)S(1)}, s32[512,1]{0,1:T(1,128)S(1)}) fusion(s32[]{:T(128)} %bitcast.19, s32[]{:T(128)} %bitcast.20, s32[]{:T(128)} %bitcast.21, s32[]{:T(128)} %bitcast.22, s32[]{:T(128)} %bitcast.23, s32[]{:T(128)} %bitcast.25, s32[]{:T(128)} %bitcast.24, s32[512,1]{0,1:T(1,128)S(1)} %bitcast.78), kind=kLoop, calls=%fused_computation.50 | loop fusion | flops 7680 | bytes 6172 | tf_op jit(solution)/shard_map/gather | solution.py:21
  44.5 5.5 %select_select_fusion = s32[512]{0:T(512)S(1)} fusion(pred[512]{0:T(512)(128)(4,1)S(1)} %get-tuple-element.91, pred[512]{0:T(512)(128)(4,1)S(1)} %get-tuple-element.90, pred[512]{0:T(512)(128)(4,1)S(1)} %get-tuple-element.89, pred[512]{0:T(512)(128)(4,1)S(1)} %get-tuple-element.88, pred[512]{0:T(512)(128)(4,1)S(1)} %get-tuple-element.87, ...), kind=kLoop, calls=%fused_computation.62 | loop fusion | flops 4608 | bytes 8740 | tf_op jit(solution)/shard_map/gather | solution.py:21
  50.2 51.2 %all-to-all-done.1 = bf16[16,32,2048]{2,1,0:T(8,128)(2,1)S(1)} async-done(((bf16[16,32,2048]{2,1,0:T(8,128)(2,1)}), bf16[16,32,2048]{2,1,0:T(8,128)(2,1)S(1)}, u32[]{:S(2)}, u32[]{:S(2)}) %all-to-all-start.1) | async-done | bytes 2097184 | tf_op jit(solution)/shard_map/all_to_all | solution.py:91
  101.4 3.3 gather_fusion.1
  104.7 60.1 %all-gather.9.cloned.1.call-done = bf16[1,2048,768]{2,1,0:T(8,128)(2,1)} async-done(((bf16[1,64,768]{2,1,0:T(8,128)(2,1)}), bf16[1,2048,768]{2,1,0:T(8,128)(2,1)}) %all-gather.9.cloned.1.call-update) | async-done | bytes 3145744 | tf_op jit(solution)/shard_map/all_gather | solution.py:97
  164.9 9.3 %while.20 = (s32[]{:T(128)}, bf16[512,768]{1,0:T(8,128)(2,1)S(1)}, s32[]{:T(128)}, bf16[512,2048]{1,0:T(8,128)(2,1)}, bf16[2048,768]{1,0:T(8,128)(2,1)}, /*index...) while((s32[]{:T(128)}, bf16[512,768]{1,0:T(8,128)(2,1)S(1)}, s32[]{:T(128)}, ...), condition=%wide.region_8.9_spmd, body=%wide.region_7.8_spmd.sunk | while | flops 805896192 | bytes 20907188 | solution.py:39
  164.9 2.8 fusion.35
  169.6 2.8 fusion.35
  174.2 60.9 %all-gather.11.cloned.1.call-done = bf16[1,768,2048]{1,2,0:T(8,128)(2,1)} async-done(((bf16[1,768,64]{1,2,0:T(8,128)(2,1)}), bf16[1,768,2048]{1,2,0:T(8,128)(2,1)}) %all-gather.11.cloned.1.call-update) | async-done | bytes 3145744 | tf_op jit(solution)/shard_map/all_gather | solution.py:98
  235.1 4.7 %copy.43 = bf16[768,2048]{1,0:T(8,128)(2,1)} copy(bf16[768,2048]{0,1:T(8,128)(2,1)} %bitcast.76) | data formatting | bytes 6291456 | tf_op jit(solution)/shard_map/while | solution.py:54
  240.0 5.0 %while.21 = (s32[]{:T(128)}, bf16[512,2048]{1,0:T(8,128)(2,1)S(1)}, s32[]{:T(128)}, bf16[512,768]{1,0:T(8,128)(2,1)S(1)}, bf16[768,2048]{1,0:T(8,128)(2,1)}, /*index=5*/s32[]{:T(128)}, s32[]{:T(128)}, s32[]{:T(128)}, s32[]{:T(128)}) while((s32[]{:T(128)}, bf16[512,2048]{1,0:T(8,128)(2,1)S(1)}, s32[]{:T(128)}, ...), condition=%wide.region_10.11_spmd, body=%wide.region_9.10_spmd.sunk | while | flops 402915328 | bytes 3867787 | solution.py:54
  240.0 2.5 fusion.39
  242.5 2.5 fusion.39
  245.0 3.3 %gather_fusion.2 = bf16[512,2048]{1,0:T(8,128)(2,1)} fusion(bf16[512,2048]{1,0:T(8,128)(2,1)S(1)} %get-tuple-element.67, s32[1024]{0:T(1024)S(1)} %pad_clamp_fusion.1), kind=kCustom, calls=%fused_computation.2 | custom fusion | bytes 4196352 | tf_op jit(solution)/shard_map/gather | solution.py:64
  248.4 3.1 broadcast_select_fusion.1
  251.5 11.1 %all-to-all-start.2 = ((bf16[16,32,2048]{2,1,0:T(8,128)(2,1)}), bf16[16,32,2048]{2,1,0:T(8,128)(2,1)S(1)}, u32[]{:S(2)}, u32[]{:S(2)}) async-start(bf16[16,32,2048]{2,1,0:T(8,128)(2,1)} %broadcast_select_fusion.1), calls=%async_computation.2 | async-start | bytes 4194304 | tf_op jit(solution)/shard_map/all_to_all | solution.py:103
  262.6 52.6 %all-to-all-done.2 = bf16[16,32,2048]{2,1,0:T(8,128)(2,1)S(1)} async-done(((bf16[16,32,2048]{2,1,0:T(8,128)(2,1)}), bf16[16,32,2048]{2,1,0:T(8,128)(2,1)S(1)}, u32[]{:S(2)}, u32[]{:S(2)}) %all-to-all-start.2) | async-done | bytes 2097184 | tf_op jit(solution)/shard_map/all_to_all | solution.py:103
  315.2 2.3 gather_fusion.3
  317.6 1.7 reshape.208
  320.8 1.8 fusion.11
  (59 shorter events, 16.6 us)
Async XLA Ops:
  6.5 16.9 %copy-start = (bf16[128,2048]{1,0:T(8,128)(2,1)S(1)}, bf16[128,2048]{1,0:T(8,128)(2,1)}, u32[]{:S(2)}) copy-start(bf16[128,2048]{1,0:T(8,128)(2,1)} %param.10) | copy-start | bytes 1572868
  6.5 98.1 %all-gather.7.cloned.1.call-start = ((), (), s32[]{:S(2)}) async-start(), calls=%async_computation.3 | async-start | bytes 3244032 | tf_op jit(solution)/shard_map/all_gather | solution.py:96
  7.3 157.6 %all-gather.9.cloned.1.call-start = ((), (), s32[]{:S(2)}) async-start(), calls=%async_computation.4 | async-start | bytes 3244032 | tf_op jit(solution)/shard_map/all_gather | solution.py:97
  10.7 19.0 %all-to-all-start = ((s32[16,1,1]{2,1,0:T(1,128)}), s32[16,1,1]{2,1,0:T(1,128)S(1)}, u32[]{:S(2)}, u32[]{:S(2)}) async-start(s32[16,1,1]{2,1,0:T(1,128)} %copy.38), calls=%async_computation | async-start | bytes 16384 | tf_op jit(solution)/shard_map/all_to_all | solution.py:92
  29.7 71.7 %all-to-all-start.1 = ((bf16[16,32,2048]{2,1,0:T(8,128)(2,1)}), bf16[16,32,2048]{2,1,0:T(8,128)(2,1)S(1)}, u32[]{:S(2)}, u32[]{:S(2)}) async-start(bf16[16,32,2048]{2,1,0:T(8,128)(2,1)} %broadcast_select_fusion), calls=%async_computation.1 | async-start | bytes 4194304 | tf_op jit(solution)/shard_map/all_to_all | solution.py:91
  36.5 198.5 %all-gather.11.cloned.1.call-start = ((), (), s32[]{:S(2)}) async-start(), calls=%async_computation.5 | async-start | bytes 3244032 | tf_op jit(solution)/shard_map/all_gather | solution.py:98
  164.9 3.0 copy-start.2
  169.6 3.0 copy-start.2
  251.5 11.1 %copy-start.1 = (f32[128,2]{0,1:T(2,128)S(1)}, f32[128,2]{0,1:T(2,128)}, u32[]{:S(2)}) copy-start(f32[128,2]{0,1:T(2,128)} %param.12) | copy-start | bytes 3076
  251.5 63.7 %all-to-all-start.2 = ((bf16[16,32,2048]{2,1,0:T(8,128)(2,1)}), bf16[16,32,2048]{2,1,0:T(8,128)(2,1)S(1)}, u32[]{:S(2)}, u32[]{:S(2)}) async-start(bf16[16,32,2048]{2,1,0:T(8,128)(2,1)} %broadcast_select_fusion.1), calls=%async_computation.2 | async-start | bytes 4194304 | tf_op jit(solution)/shard_map/all_to_all | solution.py:103
Sparse Core Ops, SparseCore 0:
  9.5 84.9 all-gather.6
  96.6 68.1 all-gather.8
  167.0 68.0 all-gather.10
where the time goes:
time: 331 us; the launch traced here: 329 us
  waiting for transfers between devices  229 us (69%)
  starting transfers between devices  28.1 us (8%)
  local copies, waits for them, and re-layouts  25.1 us (8%)
  other arithmetic  18.8 us (6%)
  between operations  14 us (4%)
  matrix products  13.8 us (4%)
    all_gather x1, waiting for transfers between devices, per_device(): lax.all_gather(down_weight[0], 'dp', axis=1, tiled=True)  60.9 us
    all_gather x1, waiting for transfers between devices, per_device(): lax.all_gather(up_weight[0], 'dp', axis=0, tiled=True)  60.1 us
    all_to_all x1, waiting for transfers between devices, per_device(): lax.all_to_all(produced, 'expert', split_axis=0, concat_axis=0, tiled=True)  52.6 us
    all_to_all x1, waiting for transfers between devices, per_device(): lax.all_to_all(outgoing, 'expert', split_axis=0, concat_axis=0, tiled=True)  51.2 us
    all_to_all x1, starting transfers between devices, per_device(): lax.all_to_all(produced, 'expert', split_axis=0, concat_axis=0, tiled=True)  11.1 us
    all_to_all x1, starting transfers between devices, per_device(): lax.all_to_all(counts, 'expert', split_axis=0, concat_axis=0, tiled=True)  10.2 us
    gather x3, other arithmetic, pack_rows(): within = packed_index - starts[source_of]  10.1 us
    all_to_all x1, starting transfers between devices, per_device(): lax.all_to_all(outgoing, 'expert', split_axis=0, concat_axis=0, tiled=True)  6.79 us
  transfers between devices with their start and end apart: 6, of which 5 were waited for; matrix products, arithmetic and copies ran while one was open for 10% of the time, Pallas kernels for 0%

commit v1 on v0

v1 whole, which is shorter than its diff:
```python
import jax
import jax.numpy as jnp
from jax import lax
from jax.experimental import pallas as pl
from jax.experimental.pallas import tpu as pltpu
from jax.sharding import PartitionSpec as P

F32 = jnp.float32
BF16 = jnp.bfloat16


def dot(a, b, dims=((1,), (0,))):
    return lax.dot_general(a, b, (dims, ((), ())), preferred_element_type=F32)


def dispatch_kernel(routes, gates, tokens, outgoing, high, low, *, capacity):
    slots = outgoing.shape[0]
    count = tokens.shape[0]
    top = routes.shape[0]
    slot = lax.broadcasted_iota(jnp.int32, (slots, count), 0)
    owner = slot // capacity
    place = (slot - owner * capacity).astype(F32)
    member = jnp.zeros((slots, count), F32)
    weight = jnp.zeros((slots, count), F32)
    for k in range(top):
        named = routes[k : k + 1, :] == owner
        member = jnp.where(named, 1.0, member)
        weight = jnp.where(named, gates[k : k + 1, :], weight)
    earlier = lax.broadcasted_iota(jnp.int32, (count, count), 0) < lax.broadcasted_iota(
        jnp.int32, (count, count), 1
    )
    rank = dot(member.astype(BF16), jnp.where(earlier, 1.0, 0.0).astype(BF16))
    chosen = jnp.where(rank == place, member, 0.0)
    outgoing[...] = dot(chosen.astype(BF16), tokens[...]).astype(BF16)
    weight = jnp.transpose(chosen * weight)
    rounded = weight.astype(BF16)
    high[...] = rounded
    low[...] = (weight - rounded.astype(F32)).astype(BF16)


def expert_kernel(rows, weights, produced, gate, up, down, hidden, sems, *, wide, shard):
    shards = weights.shape[0]
    inner = weights.shape[2]
    features = produced.shape[1]
    parts = (gate, up, down)
    copies = []
    for n in range(inner // wide):
        for p in range(2):
            copy = pltpu.make_async_copy(
                weights.at[:, p * shard : (p + 1) * shard, n * wide : (n + 1) * wide],
                parts[p].at[:, :, n * wide : (n + 1) * wide],
                sems.at[2 * n + p],
            )
            copy.start()
            copies.append(copy)
    last = pltpu.make_async_copy(
        weights.at[:, 2 * shard : 3 * shard, :], down, sems.at[2 * (inner // wide)]
    )
    last.start()
    x = rows[...]
    for n in range(inner // wide):
        columns = slice(n * wide, (n + 1) * wide)
        copies[2 * n].wait()
        copies[2 * n + 1].wait()
        gated = dot(x, gate[:, :, columns].reshape(shards * shard, wide))
        upward = dot(x, up[:, :, columns].reshape(shards * shard, wide))
        hidden[:, columns] = (gated / (1.0 + jnp.exp(-gated)) * upward).astype(BF16)
    last.wait()
    h = hidden[...]
    step = wide // shard
    for m in range(features // wide):
        part = down[m * step : (m + 1) * step].reshape(wide, inner)
        produced[:, m * wide : (m + 1) * wide] = dot(h, part, ((1,), (1,))).astype(BF16)


def combine_kernel(high, low, returned, mixture):
    rows = returned[...]
    mixture[...] = (dot(high[...], rows) + dot(low[...], rows)).astype(BF16)


def per_device(tokens, routes, gate_values, gate_weight, up_weight, down_weight):
    groups = lax.axis_size("expert")
    shards = lax.axis_size("dp")
    count, features = tokens.shape
    top = routes.shape[1]
    capacity = 2 * count * top // groups
    slots = groups * capacity
    _, shard, inner = gate_weight.shape
    joined = jnp.concatenate([gate_weight[0], up_weight[0], down_weight[0].T], axis=0)
    weights = lax.all_gather(joined, "dp", axis=0)
    outgoing, high, low = pl.pallas_call(
        lambda *refs: dispatch_kernel(*refs, capacity=capacity),
        out_shape=(
            jax.ShapeDtypeStruct((slots, features), BF16),
            jax.ShapeDtypeStruct((count, slots), BF16),
            jax.ShapeDtypeStruct((count, slots), BF16),
        ),
        name="dispatch",
    )(routes.T, gate_values.T, tokens)

    def exchange(rows):
        blocks = rows.reshape(groups, capacity, features)
        moved = lax.all_to_all(blocks, "expert", split_axis=0, concat_axis=0, tiled=True)
        return moved.reshape(slots, features)

    arrived = exchange(outgoing)
    wide = 256
    produced = pl.pallas_call(
        lambda *refs: expert_kernel(*refs, wide=wide, shard=shard),
        out_shape=jax.ShapeDtypeStruct((slots, features), BF16),
        in_specs=[
            pl.BlockSpec(memory_space=pltpu.VMEM),
            pl.BlockSpec(memory_space=pl.ANY),
        ],
        out_specs=pl.BlockSpec(memory_space=pltpu.VMEM),
        scratch_shapes=[
            pltpu.VMEM((shards, shard, inner), BF16),
            pltpu.VMEM((shards, shard, inner), BF16),
            pltpu.VMEM((shards, shard, inner), BF16),
            pltpu.VMEM((slots, inner), BF16),
            pltpu.SemaphoreType.DMA((2 * (inner // wide) + 1,)),
        ],
        name="expert",
    )(arrived, weights)
    returned = exchange(produced)
    return pl.pallas_call(
        combine_kernel,
        out_shape=jax.ShapeDtypeStruct((count, features), BF16),
        name="combine",
    )(high, low, returned)


def solution(mesh):
    placed = (
        P(("dp", "expert"), None),
        P(("dp", "expert"), None),
        P(("dp", "expert"), None),
        P("expert", "dp", None),
        P("expert", "dp", None),
        P("expert", None, "dp"),
    )
    return jax.shard_map(
        per_device, mesh=mesh, in_specs=placed, out_specs=P(("dp", "expert"), None), check_vma=False
    )
```

time: 331 us -> 208 us (0.63)
  the two profiles are of different devices: /device:TPU:1 before, /device:TPU:8 now
where the time goes in v1:
time: 208 us
  blocking collectives  138 us (66%)
  waiting for transfers between devices  37.7 us (18%)
  Pallas kernels  16.7 us (8%)
  between operations  13.4 us (6%)
    all_to_all x2, blocking collectives, exchange(): lax.all_to_all(blocks, 'expert', split_axis=0, concat_axis=0, tiled=True)  138 us
    all_gather x1, waiting for transfers between devices, per_device(): weights = lax.all_gather(joined, 'dp', axis=0)  37.7 us
    pallas_call x1, Pallas kernels, per_device(): pl.pallas_call(lambda *refs: expert_kernel(*refs, wide=wide, shard=shard)...  10.2 us
  transfers between devices with their start and end apart: 1, of which 1 were waited for; matrix products, arithmetic and copies ran while one was open for 0% of the time, Pallas kernels for 2%

profile of v1, /device:TPU:8, one launch (start us, length us, event | category | flops | bytes accessed | tf_op | source)
XLA Modules:
  0.0 207.9 jit_solution(6978403485243604150)
XLA Ops:
  6.5 0.0 all-gather.3.cloned.1.call-start
  6.5 1.7 pad_maximum_fusion
  8.3 0.0 all-gather.3.cloned.1.call-update
  8.3 3.3 %dispatch.1 = (bf16[512,2048]{1,0:T(8,128)(2,1)}, bf16[128,512]{1,0:T(8,128)(2,1)}, bf16[128,512]{1,0:T(8,128)(2,1)}) custom-call(s32[2,128]{1,0:T(2,128)} %bitcast.20, f32[2,128]{1,0:T(2,128)} %bitcast.21, bf16[128,2048]{1,0:T(8,128)(2,1)} %refs_2_.1), custom_call_target="tpu_custom_call" | custom-call | tf_op jit(solution)/shard_map/dispatch/pallas_call | solution.py:91
  11.6 77.3 %all_to_all.10 = bf16[16,32,2048]{2,1,0:T(8,128)(2,1)} all-to-all(bf16[16,32,2048]{2,1,0:T(8,128)(2,1)} %bitcast.16), channel_id=1, replica_groups=mesh['dp'=32,'expert'=16] {'expert'}, dimensions={0} | all-to-all | bytes 4194304 | tf_op jit(solution)/shard_map/all_to_all | solution.py:103
  88.9 37.7 %all-gather.3.cloned.1.call-done = bf16[6144,768]{1,0:T(8,128)(2,1)} async-done(((bf16[192,768]{1,0:T(8,128)(2,1)}), bf16[6144,768]{1,0:T(8,128)(2,1)}) %all-gather.3.cloned.1.call-update) | async-done | bytes 9437200 | tf_op jit(solution)/shard_map/all_gather | solution.py:90
  126.6 10.2 %expert.1 = bf16[512,2048]{1,0:T(8,128)(2,1)} custom-call(bf16[512,2048]{1,0:T(8,128)(2,1)} %bitcast.14, bf16[32,192,768]{2,1,0:T(8,128)(2,1)} %bitcast.12), custom_call_target="tpu_custom_call" | custom-call | tf_op jit(solution)/shard_map/expert/pallas_call | solution.py:108
  136.8 61.0 %all_to_all.11 = bf16[16,32,2048]{2,1,0:T(8,128)(2,1)} all-to-all(bf16[16,32,2048]{2,1,0:T(8,128)(2,1)} %bitcast.15), channel_id=1, replica_groups=mesh['dp'=32,'expert'=16] {'expert'}, dimensions={0} | all-to-all | bytes 4194304 | tf_op jit(solution)/shard_map/all_to_all | solution.py:103
  197.8 3.3 %combine.1 = bf16[128,2048]{1,0:T(8,128)(2,1)} custom-call(bf16[128,512]{1,0:T(8,128)(2,1)} %get-tuple-element.8.high, bf16[128,512]{1,0:T(8,128)(2,1)} %get-tuple-element.9.low, bf16[512,2048]{1,0:T(8,128)(2,1)} %bitcast.13), custom_call_target="tpu_custom_call" | custom-call | tf_op jit(solution)/shard_map/combine/pallas_call | solution.py:126
Async XLA Ops:
  6.5 120.0 %all-gather.3.cloned.1.call-start = ((), (), s32[]{:S(2)}) async-start(), calls=%async_computation.2 | async-start | bytes 9732096 | tf_op jit(solution)/shard_map/all_gather | solution.py:90
Sparse Core Ops, SparseCore 0:
  9.5 117.0 all-gather.2

commit v2 on v1

--- a/solution.py
+++ b/solution.py
@@ -38,39 +38,54 @@
     low[...] = (weight - rounded.astype(F32)).astype(BF16)
 
 
-def expert_kernel(rows, weights, produced, gate, up, down, hidden, sems, *, wide, shard):
-    shards = weights.shape[0]
-    inner = weights.shape[2]
+def expert_kernel(side, rows, weights, produced, x, gate, up, down, hidden, out, sems, *, wide, shard):
+    members = weights.shape[0]
+    inner = weights.shape[3]
     features = produced.shape[1]
-    parts = (gate, up, down)
-    copies = []
-    for n in range(inner // wide):
-        for p in range(2):
-            copy = pltpu.make_async_copy(
-                weights.at[:, p * shard : (p + 1) * shard, n * wide : (n + 1) * wide],
-                parts[p].at[:, :, n * wide : (n + 1) * wide],
-                sems.at[2 * n + p],
+    mine = side[0]
+    sem = [0]
+
+    def begin(source, target):
+        copy = pltpu.make_async_copy(source, target, sems.at[sem[0]])
+        sem[0] += 1
+        copy.start()
+        return copy
+
+    def fetch(p, target, first, size):
+        return [
+            begin(
+                weights.at[:, s, p * shard : (p + 1) * shard, first : first + size],
+                target.at[
+                    pl.ds((mine if s == 0 else 1 - mine) * members, members), :, first : first + size
+                ],
             )
-            copy.start()
-            copies.append(copy)
-    last = pltpu.make_async_copy(
-        weights.at[:, 2 * shard : 3 * shard, :], down, sems.at[2 * (inner // wide)]
-    )
-    last.start()
-    x = rows[...]
-    for n in range(inner // wide):
-        columns = slice(n * wide, (n + 1) * wide)
-        copies[2 * n].wait()
-        copies[2 * n + 1].wait()
-        gated = dot(x, gate[:, :, columns].reshape(shards * shard, wide))
-        upward = dot(x, up[:, :, columns].reshape(shards * shard, wide))
+            for s in range(2)
+        ]
+
+    arrival = begin(rows, x)
+    blocks = []
+    for first in range(0, inner, wide):
+        blocks.append(fetch(0, gate, first, wide) + fetch(1, up, first, wide))
+    last = fetch(2, down, 0, inner)
+    arrival.wait()
+    for n, first in enumerate(range(0, inner, wide)):
+        columns = slice(first, first + wide)
+        for copy in blocks[n]:
+            copy.wait()
+        gated = dot(x[...], gate[:, :, columns].reshape(2 * members * shard, wide))
+        upward = dot(x[...], up[:, :, columns].reshape(2 * members * shard, wide))
         hidden[:, columns] = (gated / (1.0 + jnp.exp(-gated)) * upward).astype(BF16)
-    last.wait()
-    h = hidden[...]
+    for copy in last:
+        copy.wait()
     step = wide // shard
+    leaving = []
     for m in range(features // wide):
+        columns = slice(m * wide, (m + 1) * wide)
         part = down[m * step : (m + 1) * step].reshape(wide, inner)
-        produced[:, m * wide : (m + 1) * wide] = dot(h, part, ((1,), (1,))).astype(BF16)
+        out[:, columns] = dot(hidden[...], part, ((1,), (1,))).astype(BF16)
+        leaving.append(begin(out.at[:, columns], produced.at[:, columns]))
+    for copy in leaving:
+        copy.wait()
 
 
 def combine_kernel(high, low, returned, mixture):
@@ -87,7 +102,12 @@
     slots = groups * capacity
     _, shard, inner = gate_weight.shape
     joined = jnp.concatenate([gate_weight[0], up_weight[0], down_weight[0].T], axis=0)
-    weights = lax.all_gather(joined, "dp", axis=0)
+    half = shards // 2
+    swap = [(d, (d + half) % shards) for d in range(shards)]
+    both = jnp.stack([joined, lax.ppermute(joined, "dp", swap)])
+    sides = [list(range(half)), list(range(half, shards))]
+    weights = lax.all_gather(both, "dp", axis=0, axis_index_groups=sides)
+    side = (lax.axis_index("dp") // half).astype(jnp.int32).reshape(1)
     outgoing, high, low = pl.pallas_call(
         lambda *refs: dispatch_kernel(*refs, capacity=capacity),
         out_shape=(
@@ -105,27 +125,36 @@
 
     arrived = exchange(outgoing)
     wide = 256
+    anywhere = pl.BlockSpec(memory_space=pl.ANY)
+    blocks = inner // wide
     produced = pl.pallas_call(
         lambda *refs: expert_kernel(*refs, wide=wide, shard=shard),
         out_shape=jax.ShapeDtypeStruct((slots, features), BF16),
-        in_specs=[
-            pl.BlockSpec(memory_space=pltpu.VMEM),
-            pl.BlockSpec(memory_space=pl.ANY),
-        ],
-        out_specs=pl.BlockSpec(memory_space=pltpu.VMEM),
+        in_specs=[pl.BlockSpec(memory_space=pltpu.SMEM), anywhere, anywhere],
+        out_specs=anywhere,
         scratch_shapes=[
+            pltpu.VMEM((slots, features), BF16),
             pltpu.VMEM((shards, shard, inner), BF16),
             pltpu.VMEM((shards, shard, inner), BF16),
             pltpu.VMEM((shards, shard, inner), BF16),
             pltpu.VMEM((slots, inner), BF16),
-            pltpu.SemaphoreType.DMA((2 * (inner // wide) + 1,)),
+            pltpu.VMEM((slots, features), BF16),
+            pltpu.SemaphoreType.DMA((1 + 4 * blocks + 2 + features // wide,)),
         ],
         name="expert",
-    )(arrived, weights)
+    )(side, arrived, weights)
     returned = exchange(produced)
+    band = 512
     return pl.pallas_call(
         combine_kernel,
         out_shape=jax.ShapeDtypeStruct((count, features), BF16),
+        grid=(features // band,),
+        in_specs=[
+            pl.BlockSpec((count, slots), lambda i: (0, 0)),
+            pl.BlockSpec((count, slots), lambda i: (0, 0)),
+            pl.BlockSpec((slots, band), lambda i: (0, i)),
+        ],
+        out_specs=pl.BlockSpec((count, band), lambda i: (0, i)),
         name="combine",
     )(high, low, returned)
 

time: 208 us -> 169 us (0.81)
  the two profiles are of different devices: /device:TPU:8 before, /device:TPU:1 now
where the time goes in v2:
time: 169 us
  waiting for transfers between devices  61.7 us (37%)
  blocking collectives  59.5 us (35%)
  Pallas kernels  16.4 us (10%)
  starting transfers between devices  15.9 us (9%)
  between operations  13.4 us (8%)
  other arithmetic  1.9 us (1%)
    all_to_all x1, blocking collectives, exchange(): lax.all_to_all(blocks, 'expert', split_axis=0, concat_axis=0, tiled=True)  59.5 us
    all_to_all x1, waiting for transfers between devices, exchange(): lax.all_to_all(blocks, 'expert', split_axis=0, concat_axis=0, tiled=True)  50.7 us
    all_to_all x1, starting transfers between devices, exchange(): lax.all_to_all(blocks, 'expert', split_axis=0, concat_axis=0, tiled=True)  11.9 us
    pallas_call x1, Pallas kernels, per_device(): pl.pallas_call(lambda *refs: expert_kernel(*refs, wide=wide, shard=shard)...  9 us
    all_gather x1, waiting for transfers between devices, per_device(): weights = lax.all_gather(both, 'dp', axis=0, axis_index_groups=sides)  6.87 us
    pallas_call x1, Pallas kernels, per_device(): pl.pallas_call(combine_kernel, out_shape=jax.ShapeDtypeStruct((count, fea...  4.12 us
    ppermute x1, waiting for transfers between devices, per_device(): both = jnp.stack([joined, lax.ppermute(joined, 'dp', swap)])  4.1 us
    ppermute x1, starting transfers between devices, per_device(): both = jnp.stack([joined, lax.ppermute(joined, 'dp', swap)])  4.02 us
  transfers between devices with their start and end apart: 3, of which 3 were waited for; matrix products, arithmetic and copies ran while one was open for 0% of the time, Pallas kernels for 2%

profile of v2, /device:TPU:1, one launch (start us, length us, event | category | flops | bytes accessed | tf_op | source)
XLA Modules:
  0.0 168.9 jit_solution(8497686081131116060)
XLA Ops:
  6.5 0.0 all-gather.3.cloned.1.call-start
  6.5 1.0 fusion
  7.6 4.0 %collective-permute-start = (bf16[192,768]{1,0:T(8,128)(2,1)S(1)}, bf16[192,768]{1,0:T(8,128)(2,1)S(1)}, u32[]{:S(2)}, u32[]{:S(2)}) collective-permute-start(bf16[192,768]{1,0:T(8,128)(2,1)S(1)} %get-tuple-element.12), channel_id=1, source_target_pairs={{0,256},{16,272},{32,288},{48,304},{64,320},{80,336},{96,352},{112... | collective-permute-start | bytes 884744 | tf_op jit(solution)/shard_map/ppermute | solution.py:107
  11.6 4.1 %collective-permute-done = bf16[192,768]{1,0:T(8,128)(2,1)S(1)} collective-permute-done((bf16[192,768]{1,0:T(8,128)(2,1)S(1)}, bf16[192,768]{1,0:T(8,128)(2,1)S(1)}, u32[]{:S(2)}, u32[]{:S(2)}) %collective-permute-start) | collective-permute-done | bytes 294944 | tf_op jit(solution)/shard_map/ppermute | solution.py:107
  15.7 0.9 pad_maximum_fusion
  16.6 0.0 all-gather.3.cloned.1.call-update
  16.6 3.3 %dispatch.1 = (bf16[512,2048]{1,0:T(8,128)(2,1)}, bf16[128,512]{1,0:T(8,128)(2,1)}, bf16[128,512]{1,0:T(8,128)(2,1)}) custom-call(s32[2,128]{1,0:T(2,128)} %bitcast.25, f32[2,128]{1,0:T(2,128)} %bitcast.26, bf16[128,2048]{1,0:T(8,128)(2,1)} %refs_2_.1), custom_call_target="tpu_custom_call" | custom-call | tf_op jit(solution)/shard_map/dispatch/pallas_call | solution.py:111
  19.9 11.9 %all-to-all-start = ((bf16[16,32,2048]{2,1,0:T(8,128)(2,1)}), bf16[16,32,2048]{2,1,0:T(8,128)(2,1)S(1)}, u32[]{:S(2)}, u32[]{:S(2)}) async-start(bf16[16,32,2048]{2,1,0:T(8,128)(2,1)} %bitcast.20), calls=%async_computation | async-start | bytes 4194304 | tf_op jit(solution)/shard_map/all_to_all | solution.py:123
  31.8 50.7 %all-to-all-done = bf16[16,32,2048]{2,1,0:T(8,128)(2,1)S(1)} async-done(((bf16[16,32,2048]{2,1,0:T(8,128)(2,1)}), bf16[16,32,2048]{2,1,0:T(8,128)(2,1)S(1)}, u32[]{:S(2)}, u32[]{:S(2)}) %all-to-all-start) | async-done | bytes 2097184 | tf_op jit(solution)/shard_map/all_to_all | solution.py:123
  82.5 0.0 copy-start
  82.5 6.9 %all-gather.3.cloned.1.call-done = bf16[32,192,768]{2,1,0:T(8,128)(2,1)} async-done(((bf16[2,192,768]{2,1,0:T(8,128)(2,1)}), bf16[32,192,768]{2,1,0:T(8,128)(2,1)}) %all-gather.3.cloned.1.call-update) | async-done | bytes 9437200 | tf_op jit(solution)/shard_map/all_gather | solution.py:109
  89.4 0.0 copy-done
  89.4 9.0 %expert.1 = bf16[512,2048]{1,0:T(8,128)(2,1)} custom-call(s32[1]{0:T(128)} %bitcast.2.refs_0_, bf16[512,2048]{1,0:T(8,128)(2,1)} %bitcast.18, bf16[16,2,192,768]{3,2,1,0:T(8,128)(2,1)} %bitcast.16), custom_call_target="tpu_custom_call" | custom-call | tf_op jit(solution)/shard_map/expert/pallas_call | solution.py:130
  98.4 59.5 %all_to_all.10 = bf16[16,32,2048]{2,1,0:T(8,128)(2,1)} all-to-all(bf16[16,32,2048]{2,1,0:T(8,128)(2,1)} %bitcast.19), channel_id=1, replica_groups=mesh['dp'=32,'expert'=16] {'expert'}, dimensions={0} | all-to-all | bytes 4194304 | tf_op jit(solution)/shard_map/all_to_all | solution.py:123
  157.9 4.1 %combine.1 = bf16[128,2048]{1,0:T(8,128)(2,1)} custom-call(bf16[128,512]{1,0:T(8,128)(2,1)} %get-tuple-element.8.high, bf16[128,512]{1,0:T(8,128)(2,1)} %get-tuple-element.9.low, bf16[512,2048]{1,0:T(8,128)(2,1)} %bitcast.17), custom_call_target="tpu_custom_call" | custom-call | tf_op jit(solution)/shard_map/combine/pallas_call | solution.py:148
Async XLA Ops:
  6.5 82.8 %all-gather.3.cloned.1.call-start = ((), (), s32[]{:S(2)}) async-start(), calls=%async_computation.2 | async-start | bytes 10027008 | tf_op jit(solution)/shard_map/all_gather | solution.py:109
  7.6 8.1 %collective-permute-start = (bf16[192,768]{1,0:T(8,128)(2,1)S(1)}, bf16[192,768]{1,0:T(8,128)(2,1)S(1)}, u32[]{:S(2)}, u32[]{:S(2)}) collective-permute-start(bf16[192,768]{1,0:T(8,128)(2,1)S(1)} %get-tuple-element.12), channel_id=1, source_target_pairs={{0,256},{16,272},{32,288},{48,304},{64,320},{80,336},{96,352},{112... | collective-permute-start | bytes 884744 | tf_op jit(solution)/shard_map/ppermute | solution.py:107
  19.9 62.6 %all-to-all-start = ((bf16[16,32,2048]{2,1,0:T(8,128)(2,1)}), bf16[16,32,2048]{2,1,0:T(8,128)(2,1)S(1)}, u32[]{:S(2)}, u32[]{:S(2)}) async-start(bf16[16,32,2048]{2,1,0:T(8,128)(2,1)} %bitcast.20), calls=%async_computation | async-start | bytes 4194304 | tf_op jit(solution)/shard_map/all_to_all | solution.py:123
  82.5 6.9 %copy-start = (bf16[16,32,2048]{2,1,0:T(8,128)(2,1)}, bf16[16,32,2048]{2,1,0:T(8,128)(2,1)S(1)}, u32[]{:S(2)}) copy-start(bf16[16,32,2048]{2,1,0:T(8,128)(2,1)S(1)} %all-to-all-done) | copy-start | bytes 6291460
Sparse Core Ops, SparseCore 0:
  16.7 72.5 all-gather.2

commit v3 on v2

--- a/solution.py
+++ b/solution.py
@@ -13,7 +13,7 @@
     return lax.dot_general(a, b, (dims, ((), ())), preferred_element_type=F32)
 
 
-def dispatch_kernel(routes, gates, tokens, outgoing, high, low, *, capacity):
+def dispatch_kernel(routes, gates, tokens, outgoing, factors, *, capacity):
     slots = outgoing.shape[0]
     count = tokens.shape[0]
     top = routes.shape[0]
@@ -34,15 +34,17 @@
     outgoing[...] = dot(chosen.astype(BF16), tokens[...]).astype(BF16)
     weight = jnp.transpose(chosen * weight)
     rounded = weight.astype(BF16)
-    high[...] = rounded
-    low[...] = (weight - rounded.astype(F32)).astype(BF16)
+    factors[:count, :] = rounded
+    factors[count:, :] = (weight - rounded.astype(F32)).astype(BF16)
 
 
-def expert_kernel(side, rows, weights, produced, x, gate, up, down, hidden, out, sems, *, wide, shard):
+def expert_kernel(
+    place, rows, weights, near, far, produced, x, gate, up, down, hidden, out, sems, *, wide, shard, ring
+):
     members = weights.shape[0]
     inner = weights.shape[3]
     features = produced.shape[1]
-    mine = side[0]
+    mine, z, core = place[0], place[1], place[2]
     sem = [0]
 
     def begin(source, target):
@@ -51,13 +53,14 @@
         copy.start()
         return copy
 
-    def fetch(p, target, first, size):
+    def side(s):
+        return mine if s == 0 else 1 - mine
+
+    def fetch(p, target, first):
         return [
             begin(
-                weights.at[:, s, p * shard : (p + 1) * shard, first : first + size],
-                target.at[
-                    pl.ds((mine if s == 0 else 1 - mine) * members, members), :, first : first + size
-                ],
+                weights.at[:, s, p * shard : (p + 1) * shard, first : first + wide],
+                target.at[pl.ds(side(s) * members, members), :, first : first + wide],
             )
             for s in range(2)
         ]
@@ -65,8 +68,14 @@
     arrival = begin(rows, x)
     blocks = []
     for first in range(0, inner, wide):
-        blocks.append(fetch(0, gate, first, wide) + fetch(1, up, first, wide))
-    last = fetch(2, down, 0, inner)
+        blocks.append(fetch(0, gate, first) + fetch(1, up, first))
+    last = []
+    for o in range(ring):
+        from_z = lax.rem(z + (ring - o), ring)
+        for source, from_core in ((near, core), (far, 1 - core)):
+            for s in range(2):
+                block = side(s) * members + from_z * 2 + from_core
+                last.append(begin(source.at[o, s], down.at[block]))
     arrival.wait()
     for n, first in enumerate(range(0, inner, wide)):
         columns = slice(first, first + wide)
@@ -88,9 +97,10 @@
         copy.wait()
 
 
-def combine_kernel(high, low, returned, mixture):
-    rows = returned[...]
-    mixture[...] = (dot(high[...], rows) + dot(low[...], rows)).astype(BF16)
+def combine_kernel(factors, returned, mixture):
+    count = mixture.shape[0]
+    sums = dot(factors[...], returned[...])
+    mixture[...] = (sums[:count] + sums[count:]).astype(BF16)
 
 
 def per_device(tokens, routes, gate_values, gate_weight, up_weight, down_weight):
@@ -101,22 +111,39 @@
     capacity = 2 * count * top // groups
     slots = groups * capacity
     _, shard, inner = gate_weight.shape
+    half = shards // 2
+    ring = half // 2
     joined = jnp.concatenate([gate_weight[0], up_weight[0], down_weight[0].T], axis=0)
-    half = shards // 2
     swap = [(d, (d + half) % shards) for d in range(shards)]
-    both = jnp.stack([joined, lax.ppermute(joined, "dp", swap)])
-    sides = [list(range(half)), list(range(half, shards))]
-    weights = lax.all_gather(both, "dp", axis=0, axis_index_groups=sides)
-    side = (lax.axis_index("dp") // half).astype(jnp.int32).reshape(1)
-    outgoing, high, low = pl.pallas_call(
+    other = lax.ppermute(joined, "dp", swap)
+    outgoing, factors = pl.pallas_call(
         lambda *refs: dispatch_kernel(*refs, capacity=capacity),
         out_shape=(
             jax.ShapeDtypeStruct((slots, features), BF16),
-            jax.ShapeDtypeStruct((count, slots), BF16),
-            jax.ShapeDtypeStruct((count, slots), BF16),
+            jax.ShapeDtypeStruct((2 * count, slots), BF16),
         ),
         name="dispatch",
     )(routes.T, gate_values.T, tokens)
+    other, outgoing = lax.optimization_barrier((other, outgoing))
+    sides = [list(range(half)), list(range(half, shards))]
+    both = jnp.stack([joined[: 2 * shard], other[: 2 * shard]])
+    weights = lax.all_gather(both, "dp", axis=0, axis_index_groups=sides)
+    own = jnp.stack([joined[2 * shard :], other[2 * shard :]])
+
+    def along(step):
+        return [
+            (d, d // half * half + (d % half // 2 + step) % ring * 2 + d % 2) for d in range(shards)
+        ]
+
+    ahead, behind = [own], [own]
+    for k in range(ring // 2):
+        ahead.append(lax.ppermute(ahead[-1], "dp", along(1)))
+        if k < ring // 2 - 1:
+            behind.append(lax.ppermute(behind[-1], "dp", along(-1)))
+    near = jnp.stack(ahead + behind[:0:-1])
+    far = lax.ppermute(near, "dp", [(d, d ^ 1) for d in range(shards)])
+    index = lax.axis_index("dp").astype(jnp.int32)
+    place = jnp.stack([index // half, index % half // 2, index % 2])
 
     def exchange(rows):
         blocks = rows.reshape(groups, capacity, features)
@@ -127,10 +154,12 @@
     wide = 256
     anywhere = pl.BlockSpec(memory_space=pl.ANY)
     blocks = inner // wide
+    anywhere = pl.BlockSpec(memory_space=pl.ANY)
+    blocks = inner // wide
     produced = pl.pallas_call(
-        lambda *refs: expert_kernel(*refs, wide=wide, shard=shard),
+        lambda *refs: expert_kernel(*refs, wide=wide, shard=shard, ring=ring),
         out_shape=jax.ShapeDtypeStruct((slots, features), BF16),
-        in_specs=[pl.BlockSpec(memory_space=pltpu.SMEM), anywhere, anywhere],
+        in_specs=[pl.BlockSpec(memory_space=pltpu.SMEM)] + [anywhere] * 4,
         out_specs=anywhere,
         scratch_shapes=[
             pltpu.VMEM((slots, features), BF16),
@@ -139,24 +168,16 @@
             pltpu.VMEM((shards, shard, inner), BF16),
             pltpu.VMEM((slots, inner), BF16),
             pltpu.VMEM((slots, features), BF16),
-            pltpu.SemaphoreType.DMA((1 + 4 * blocks + 2 + features // wide,)),
+            pltpu.SemaphoreType.DMA((1 + 4 * blocks + shards + features // wide,)),
         ],
         name="expert",
-    )(side, arrived, weights)
+    )(place, arrived, weights, near, far)
     returned = exchange(produced)
-    band = 512
     return pl.pallas_call(
         combine_kernel,
         out_shape=jax.ShapeDtypeStruct((count, features), BF16),
-        grid=(features // band,),
-        in_specs=[
-            pl.BlockSpec((count, slots), lambda i: (0, 0)),
-            pl.BlockSpec((count, slots), lambda i: (0, 0)),
-            pl.BlockSpec((slots, band), lambda i: (0, i)),
-        ],
-        out_specs=pl.BlockSpec((count, band), lambda i: (0, i)),
         name="combine",
-    )(high, low, returned)
+    )(factors, returned)
 
 
 def solution(mesh):

time: 169 us -> 177 us (1.047)
  waiting for transfers between devices: 61.7 us -> 21 us
  starting transfers between devices: 15.9 us -> 55.2 us
  local copies, waits for them, and re-layouts: 0.01 us -> 6.29 us
  other arithmetic: 1.9 us -> 4.11 us
    all_to_all x1, waiting for transfers between devices: 50.7 us -> 0.01 us  [exchange(): lax.all_to_all(blocks, 'expert', split_axis=0, concat_axis=0, tiled=True)]
    ppermute x1 -> x9, starting transfers between devices: 4.02 us -> 43.4 us  [the longest x3 20.5 us: per_device(): behind.append(lax.ppermute(behind[-1], 'dp', along(-1)))]
    ppermute x1 -> x9, waiting for transfers between devices: 4.1 us -> 21 us  [the longest x4 15.2 us: per_device(): ahead.append(lax.ppermute(ahead[-1], 'dp', along(1)))]
    all_gather x1, waiting for transfers between devices: 6.87 us -> 0.01 us  [per_device(): weights = lax.all_gather(both, 'dp', axis=0, axis_index_groups=sides)]
    unnamed x2 -> x10, local copies, waits for them, and re-layouts: 0.01 us -> 5.57 us
  transfers between devices with their start and end apart: 3 -> 11, of which waited for: 3 -> 7; matrix products, arithmetic and copies ran while one was open for 0% -> 4% of each run, Pallas kernels for 2% -> 2%
where the time goes in v3:
time: 177 us
  blocking collectives  59.8 us (34%)
  starting transfers between devices  55.2 us (31%)
  waiting for transfers between devices  21 us (12%)
  Pallas kernels  16.6 us (9%)
  between operations  13.6 us (8%)
  local copies, waits for them, and re-layouts  6.29 us (4%)
  other arithmetic  4.11 us (2%)
    all_to_all x1, blocking collectives, exchange(): lax.all_to_all(blocks, 'expert', split_axis=0, concat_axis=0, tiled=True)  59.8 us
    ppermute x3, starting transfers between devices, per_device(): behind.append(lax.ppermute(behind[-1], 'dp', along(-1)))  20.5 us
    ppermute x4, waiting for transfers between devices, per_device(): ahead.append(lax.ppermute(ahead[-1], 'dp', along(1)))  15.2 us
    all_to_all x1, starting transfers between devices, exchange(): lax.all_to_all(blocks, 'expert', split_axis=0, concat_axis=0, tiled=True)  11.8 us
    pallas_call x1, Pallas kernels, per_device(): pl.pallas_call(lambda *refs: expert_kernel(*refs, wide=wide, shard=shard,...  10.1 us
    ppermute x4, starting transfers between devices, per_device(): ahead.append(lax.ppermute(ahead[-1], 'dp', along(1)))  9.73 us
    ppermute x1, starting transfers between devices, per_device(): far = lax.ppermute(near, 'dp', [(d, d ^ 1) for d in range(shards)])  9.15 us
    unnamed x10, local copies, waits for them, and re-layouts  5.57 us
  transfers between devices with their start and end apart: 11, of which 7 were waited for; matrix products, arithmetic and copies ran while one was open for 4% of the time, Pallas kernels for 2%

profile of v3, /device:TPU:1, one launch (start us, length us, event | category | flops | bytes accessed | tf_op | source)
XLA Modules:
  0.0 176.6 jit_solution(630055007006639504)
XLA Ops:
  6.5 1.0 pad_maximum_fusion.1
  7.5 4.0 %collective-permute-start = (bf16[192,768]{1,0:T(8,128)(2,1)S(1)}, bf16[192,768]{1,0:T(8,128)(2,1)S(1)}, u32[]{:S(2)}, u32[]{:S(2)}) collective-permute-start(bf16[192,768]{1,0:T(8,128)(2,1)S(1)} %pad_maximum_fusion.1), channel_id=1, source_target_pairs={{0,256},{16,272},{32,288},{48,304},{64,320},{80,336},{96,352},{112... | collective-permute-start | bytes 884744 | tf_op jit(solution)/shard_map/ppermute | solution.py:118
  11.6 3.3 %dispatch.1 = (bf16[512,2048]{1,0:T(8,128)(2,1)}, bf16[256,512]{1,0:T(8,128)(2,1)}) custom-call(s32[2,128]{1,0:T(2,128)} %bitcast.51, f32[2,128]{1,0:T(2,128)} %bitcast.52, bf16[128,2048]{1,0:T(8,128)(2,1)} %refs_2_.1), custom_call_target="tpu_custom_call" | custom-call | tf_op jit(solution)/shard_map/dispatch/pallas_call | solution.py:119
  14.9 1.0 maximum_bitcast_fusion
  16.7 11.8 %all-to-all-start = ((bf16[16,32,2048]{2,1,0:T(8,128)(2,1)}), bf16[16,32,2048]{2,1,0:T(8,128)(2,1)S(1)}, u32[]{:S(2)}, u32[]{:S(2)}) async-start(bf16[16,32,2048]{2,1,0:T(8,128)(2,1)} %bitcast.43), calls=%async_computation | async-start | bytes 4194304 | tf_op jit(solution)/shard_map/all_to_all | solution.py:150
  28.6 4.0 %collective-permute-start.1 = (bf16[2,64,768]{2,1,0:T(8,128)(2,1)S(1)}, bf16[2,64,768]{2,1,0:T(8,128)(2,1)S(1)}, u32[]{:S(2)}, u32[]{:S(2)}) collective-permute-start(bf16[2,64,768]{2,1,0:T(8,128)(2,1)S(1)} %pad_maximum_fusion.2), channel_id=1, source_target_pairs={{0,32},{16,48},{32,64},{48,80},{64,96},{80,112},{96,128},{112,144}... | collective-permute-start | bytes 589832 | tf_op jit(solution)/shard_map/ppermute | solution.py:140
  32.6 8.6 %collective-permute-start.5 = (bf16[2,64,768]{2,1,0:T(8,128)(2,1)S(1)}, bf16[2,64,768]{2,1,0:T(8,128)(2,1)S(1)}, u32[]{:S(2)}, u32[]{:S(2)}) collective-permute-start(bf16[2,64,768]{2,1,0:T(8,128)(2,1)S(1)} %pad_maximum_fusion.2), channel_id=1, source_target_pairs={{0,224},{16,240},{32,0},{48,16},{64,32},{80,48},{96,64},{112,80},{... | collective-permute-start | bytes 589832 | tf_op jit(solution)/shard_map/ppermute | solution.py:142
  41.9 0.8 collective-permute-done.1
  42.7 1.9 %collective-permute-start.2 = (bf16[2,64,768]{2,1,0:T(8,128)(2,1)S(1)}, bf16[2,64,768]{2,1,0:T(8,128)(2,1)S(1)}, u32[]{:S(2)}, u32[]{:S(2)}) collective-permute-start(bf16[2,64,768]{2,1,0:T(8,128)(2,1)S(1)} %collective-permute-done.1), channel_id=1, source_target_pairs={{0,32},{16,48},{32,64},{48,80},{64,96},{80,112},{96,128},{112,144}... | collective-permute-start | bytes 589832 | tf_op jit(solution)/shard_map/ppermute | solution.py:140
  44.6 1.4 collective-permute-done.5
  46.1 6.2 %collective-permute-start.6 = (bf16[2,64,768]{2,1,0:T(8,128)(2,1)S(1)}, bf16[2,64,768]{2,1,0:T(8,128)(2,1)S(1)}, u32[]{:S(2)}, u32[]{:S(2)}) collective-permute-start(bf16[2,64,768]{2,1,0:T(8,128)(2,1)S(1)} %collective-permute-done.5), channel_id=1, source_target_pairs={{0,224},{16,240},{32,0},{48,16},{64,32},{80,48},{96,64},{112,80},{... | collective-permute-start | bytes 589832 | tf_op jit(solution)/shard_map/ppermute | solution.py:142
  53.0 2.2 %collective-permute-done.2 = bf16[2,64,768]{2,1,0:T(8,128)(2,1)S(1)} collective-permute-done((bf16[2,64,768]{2,1,0:T(8,128)(2,1)S(1)}, bf16[2,64,768]{2,1,0:T(8,128)(2,1)S(1)}, u32[]{:S(2)}, u32[]{:S(2)}) %collective-permute-start.2) | collective-permute-done | bytes 196640 | tf_op jit(solution)/shard_map/ppermute | solution.py:140
  55.2 1.9 %collective-permute-start.3 = (bf16[2,64,768]{2,1,0:T(8,128)(2,1)S(1)}, bf16[2,64,768]{2,1,0:T(8,128)(2,1)S(1)}, u32[]{:S(2)}, u32[]{:S(2)}) collective-permute-start(bf16[2,64,768]{2,1,0:T(8,128)(2,1)S(1)} %collective-permute-done.2), channel_id=1, source_target_pairs={{0,32},{16,48},{32,64},{48,80},{64,96},{80,112},{96,128},{112,144}... | collective-permute-start | bytes 589832 | tf_op jit(solution)/shard_map/ppermute | solution.py:140
  57.1 1.7 collective-permute-done.6
  58.7 5.7 %collective-permute-start.7 = (bf16[2,64,768]{2,1,0:T(8,128)(2,1)S(1)}, bf16[2,64,768]{2,1,0:T(8,128)(2,1)S(1)}, u32[]{:S(2)}, u32[]{:S(2)}) collective-permute-start(bf16[2,64,768]{2,1,0:T(8,128)(2,1)S(1)} %collective-permute-done.6), channel_id=1, source_target_pairs={{0,224},{16,240},{32,0},{48,16},{64,32},{80,48},{96,64},{112,80},{... | collective-permute-start | bytes 589832 | tf_op jit(solution)/shard_map/ppermute | solution.py:142
  65.1 2.3 %collective-permute-done.3 = bf16[2,64,768]{2,1,0:T(8,128)(2,1)S(1)} collective-permute-done((bf16[2,64,768]{2,1,0:T(8,128)(2,1)S(1)}, bf16[2,64,768]{2,1,0:T(8,128)(2,1)S(1)}, u32[]{:S(2)}, u32[]{:S(2)}) %collective-permute-start.3) | collective-permute-done | bytes 196640 | tf_op jit(solution)/shard_map/ppermute | solution.py:140
  67.4 1.9 %collective-permute-start.4 = (bf16[2,64,768]{2,1,0:T(8,128)(2,1)S(1)}, bf16[2,64,768]{2,1,0:T(8,128)(2,1)S(1)}, u32[]{:S(2)}, u32[]{:S(2)}) collective-permute-start(bf16[2,64,768]{2,1,0:T(8,128)(2,1)S(1)} %collective-permute-done.3), channel_id=1, source_target_pairs={{0,32},{16,48},{32,64},{48,80},{64,96},{80,112},{96,128},{112,144}... | collective-permute-start | bytes 589832 | tf_op jit(solution)/shard_map/ppermute | solution.py:140
  70.1 9.9 %collective-permute-done.4 = bf16[2,64,768]{2,1,0:T(8,128)(2,1)S(1)} collective-permute-done((bf16[2,64,768]{2,1,0:T(8,128)(2,1)S(1)}, bf16[2,64,768]{2,1,0:T(8,128)(2,1)S(1)}, u32[]{:S(2)}, u32[]{:S(2)}) %collective-permute-start.4) | collective-permute-done | bytes 196640 | tf_op jit(solution)/shard_map/ppermute | solution.py:140
  82.8 9.1 %collective-permute-start.8 = (bf16[8,2,64,768]{3,2,1,0:T(8,128)(2,1)}, bf16[8,2,64,768]{3,2,1,0:T(8,128)(2,1)}, u32[]{:S(2)}, u32[]{:S(2)}) collective-permute-start(bf16[8,2,64,768]{3,2,1,0:T(8,128)(2,1)} %bitcast_dynamic-update-slice_fusion.refs_3_), channel_id=1, source_target_pairs={{0,16},{16,0},{32,48},{48,32},{64,80},{80,64},{96,112},{112,96},{1... | collective-permute-start | bytes 4718600 | tf_op jit(solution)/shard_map/ppermute | solution.py:144
  92.6 2.7 %collective-permute-done.8.refs_4_ = bf16[8,2,64,768]{3,2,1,0:T(8,128)(2,1)} collective-permute-done((bf16[8,2,64,768]{3,2,1,0:T(8,128)(2,1)}, bf16[8,2,64,768]{3,2,1,0:T(8,128)(2,1)}, u32[]{:S(2)}, u32[]{:S(2)}) %collective-permute-start.8) | collective-permute-done | bytes 1572896 | tf_op jit(solution)/shard_map/ppermute | solution.py:144
  95.3 1.4 copy-done
  96.7 10.1 %expert.1 = bf16[512,2048]{1,0:T(8,128)(2,1)} custom-call(s32[3]{0:T(128)} %pad_add_fusion.refs_0_, bf16[512,2048]{1,0:T(8,128)(2,1)} %bitcast.40, bf16[16,2,128,768]{3,2,1,0:T(8,128)(2,1)} %bitcast.42, bf16[8,2,64,768]{3,2,1,0:T(8,128)(2,1)} %bitcast_dynamic-update-slice_fusion.refs_3_, bf16[8,2,64,768]{3,2,1,0:T(8,128)(2,1)} %collective-permute-done.8.refs_4_), custom_call_target="tpu_custom_call" | custom-call | tf_op jit(solution)/shard_map/expert/pallas_call | solution.py:159
  106.7 59.8 %all_to_all.10 = bf16[16,32,2048]{2,1,0:T(8,128)(2,1)} all-to-all(bf16[16,32,2048]{2,1,0:T(8,128)(2,1)} %bitcast.41), channel_id=1, replica_groups=mesh['dp'=32,'expert'=16] {'expert'}, dimensions={0} | all-to-all | bytes 4194304 | tf_op jit(solution)/shard_map/all_to_all | solution.py:150
  166.5 3.2 %combine.1 = bf16[128,2048]{1,0:T(8,128)(2,1)} custom-call(bf16[256,512]{1,0:T(8,128)(2,1)} %get-tuple-element.9.factors, bf16[512,2048]{1,0:T(8,128)(2,1)} %bitcast.39), custom_call_target="tpu_custom_call" | custom-call | tf_op jit(solution)/shard_map/combine/pallas_call | solution.py:176
  (22 shorter events, 7.1 us)
Async XLA Ops:
  6.5 88.7 %all-gather.3.cloned.1.call-start = ((), (), s32[]{:S(2)}) async-start(), calls=%async_computation.2 | async-start | bytes 6684672 | tf_op jit(solution)/shard_map/all_gather | solution.py:130
  7.5 8.3 %collective-permute-start = (bf16[192,768]{1,0:T(8,128)(2,1)S(1)}, bf16[192,768]{1,0:T(8,128)(2,1)S(1)}, u32[]{:S(2)}, u32[]{:S(2)}) collective-permute-start(bf16[192,768]{1,0:T(8,128)(2,1)S(1)} %pad_maximum_fusion.1), channel_id=1, source_target_pairs={{0,256},{16,272},{32,288},{48,304},{64,320},{80,336},{96,352},{112... | collective-permute-start | bytes 884744 | tf_op jit(solution)/shard_map/ppermute | solution.py:118
  16.7 11.8 %copy-start.1 = (bf16[1,768,64]{1,2,0:T(8,128)(2,1)S(1)}, bf16[1,768,64]{1,2,0:T(8,128)(2,1)}, u32[]{:S(2)}) copy-start(bf16[1,768,64]{1,2,0:T(8,128)(2,1)} %param.11) | copy-start | bytes 294916
  16.7 78.5 %all-to-all-start = ((bf16[16,32,2048]{2,1,0:T(8,128)(2,1)}), bf16[16,32,2048]{2,1,0:T(8,128)(2,1)S(1)}, u32[]{:S(2)}, u32[]{:S(2)}) async-start(bf16[16,32,2048]{2,1,0:T(8,128)(2,1)} %bitcast.43), calls=%async_computation | async-start | bytes 4194304 | tf_op jit(solution)/shard_map/all_to_all | solution.py:150
  28.6 14.1 %collective-permute-start.1 = (bf16[2,64,768]{2,1,0:T(8,128)(2,1)S(1)}, bf16[2,64,768]{2,1,0:T(8,128)(2,1)S(1)}, u32[]{:S(2)}, u32[]{:S(2)}) collective-permute-start(bf16[2,64,768]{2,1,0:T(8,128)(2,1)S(1)} %pad_maximum_fusion.2), channel_id=1, source_target_pairs={{0,32},{16,48},{32,64},{48,80},{64,96},{80,112},{96,128},{112,144}... | collective-permute-start | bytes 589832 | tf_op jit(solution)/shard_map/ppermute | solution.py:140
  32.6 13.5 %collective-permute-start.5 = (bf16[2,64,768]{2,1,0:T(8,128)(2,1)S(1)}, bf16[2,64,768]{2,1,0:T(8,128)(2,1)S(1)}, u32[]{:S(2)}, u32[]{:S(2)}) collective-permute-start(bf16[2,64,768]{2,1,0:T(8,128)(2,1)S(1)} %pad_maximum_fusion.2), channel_id=1, source_target_pairs={{0,224},{16,240},{32,0},{48,16},{64,32},{80,48},{96,64},{112,80},{... | collective-permute-start | bytes 589832 | tf_op jit(solution)/shard_map/ppermute | solution.py:142
  42.7 12.5 %collective-permute-start.2 = (bf16[2,64,768]{2,1,0:T(8,128)(2,1)S(1)}, bf16[2,64,768]{2,1,0:T(8,128)(2,1)S(1)}, u32[]{:S(2)}, u32[]{:S(2)}) collective-permute-start(bf16[2,64,768]{2,1,0:T(8,128)(2,1)S(1)} %collective-permute-done.1), channel_id=1, source_target_pairs={{0,32},{16,48},{32,64},{48,80},{64,96},{80,112},{96,128},{112,144}... | collective-permute-start | bytes 589832 | tf_op jit(solution)/shard_map/ppermute | solution.py:140
  46.1 12.7 %collective-permute-start.6 = (bf16[2,64,768]{2,1,0:T(8,128)(2,1)S(1)}, bf16[2,64,768]{2,1,0:T(8,128)(2,1)S(1)}, u32[]{:S(2)}, u32[]{:S(2)}) collective-permute-start(bf16[2,64,768]{2,1,0:T(8,128)(2,1)S(1)} %collective-permute-done.5), channel_id=1, source_target_pairs={{0,224},{16,240},{32,0},{48,16},{64,32},{80,48},{96,64},{112,80},{... | collective-permute-start | bytes 589832 | tf_op jit(solution)/shard_map/ppermute | solution.py:142
  55.2 12.3 %collective-permute-start.3 = (bf16[2,64,768]{2,1,0:T(8,128)(2,1)S(1)}, bf16[2,64,768]{2,1,0:T(8,128)(2,1)S(1)}, u32[]{:S(2)}, u32[]{:S(2)}) collective-permute-start(bf16[2,64,768]{2,1,0:T(8,128)(2,1)S(1)} %collective-permute-done.2), channel_id=1, source_target_pairs={{0,32},{16,48},{32,64},{48,80},{64,96},{80,112},{96,128},{112,144}... | collective-permute-start | bytes 589832 | tf_op jit(solution)/shard_map/ppermute | solution.py:140
  58.7 21.9 %collective-permute-start.7 = (bf16[2,64,768]{2,1,0:T(8,128)(2,1)S(1)}, bf16[2,64,768]{2,1,0:T(8,128)(2,1)S(1)}, u32[]{:S(2)}, u32[]{:S(2)}) collective-permute-start(bf16[2,64,768]{2,1,0:T(8,128)(2,1)S(1)} %collective-permute-done.6), channel_id=1, source_target_pairs={{0,224},{16,240},{32,0},{48,16},{64,32},{80,48},{96,64},{112,80},{... | collective-permute-start | bytes 589832 | tf_op jit(solution)/shard_map/ppermute | solution.py:142
  67.4 12.6 %collective-permute-start.4 = (bf16[2,64,768]{2,1,0:T(8,128)(2,1)S(1)}, bf16[2,64,768]{2,1,0:T(8,128)(2,1)S(1)}, u32[]{:S(2)}, u32[]{:S(2)}) collective-permute-start(bf16[2,64,768]{2,1,0:T(8,128)(2,1)S(1)} %collective-permute-done.3), channel_id=1, source_target_pairs={{0,32},{16,48},{32,64},{48,80},{64,96},{80,112},{96,128},{112,144}... | collective-permute-start | bytes 589832 | tf_op jit(solution)/shard_map/ppermute | solution.py:140
  82.8 12.5 %collective-permute-start.8 = (bf16[8,2,64,768]{3,2,1,0:T(8,128)(2,1)}, bf16[8,2,64,768]{3,2,1,0:T(8,128)(2,1)}, u32[]{:S(2)}, u32[]{:S(2)}) collective-permute-start(bf16[8,2,64,768]{3,2,1,0:T(8,128)(2,1)} %bitcast_dynamic-update-slice_fusion.refs_3_), channel_id=1, source_target_pairs={{0,16},{16,0},{32,48},{48,32},{64,80},{80,64},{96,112},{112,96},{1... | collective-permute-start | bytes 4718600 | tf_op jit(solution)/shard_map/ppermute | solution.py:144
  95.3 1.4 copy-start
Sparse Core Ops, SparseCore 0:
  16.8 71.6 all-gather.2

commit v4 on v3

v4 whole, which is shorter than its diff:
```python
import jax
import jax.numpy as jnp
from jax import lax
from jax.experimental import pallas as pl
from jax.experimental.pallas import tpu as pltpu
from jax.sharding import PartitionSpec as P

F32 = jnp.float32
BF16 = jnp.bfloat16


def dot(a, b, dims=((1,), (0,))):
    return lax.dot_general(a, b, (dims, ((), ())), preferred_element_type=F32)


def dispatch_kernel(routes, gates, tokens, outgoing, factors, *, capacity):
    slots = outgoing.shape[0]
    count = tokens.shape[0]
    top = routes.shape[0]
    slot = lax.broadcasted_iota(jnp.int32, (slots, count), 0)
    owner = slot // capacity
    place = (slot - owner * capacity).astype(F32)
    member = jnp.zeros((slots, count), F32)
    weight = jnp.zeros((slots, count), F32)
    for k in range(top):
        named = routes[k : k + 1, :] == owner
        member = jnp.where(named, 1.0, member)
        weight = jnp.where(named, gates[k : k + 1, :], weight)
    earlier = lax.broadcasted_iota(jnp.int32, (count, count), 0) < lax.broadcasted_iota(
        jnp.int32, (count, count), 1
    )
    rank = dot(member.astype(BF16), jnp.where(earlier, 1.0, 0.0).astype(BF16))
    chosen = jnp.where(rank == place, member, 0.0)
    outgoing[...] = dot(chosen.astype(BF16), tokens[...]).astype(BF16)
    weight = jnp.transpose(chosen * weight)
    rounded = weight.astype(BF16)
    factors[:count, :] = rounded
    factors[count:, :] = (weight - rounded.astype(F32)).astype(BF16)


def start_copy(source, target, sems, used):
    copy = pltpu.make_async_copy(source, target, sems.at[len(used)])
    copy.start()
    used.append(copy)
    return copy


def project(hidden, down, out, produced, sems, used, wide):
    inner = down.shape[2]
    step = wide // down.shape[1]
    leaving = []
    for m in range(produced.shape[1] // wide):
        columns = slice(m * wide, (m + 1) * wide)
        part = down[m * step : (m + 1) * step].reshape(wide, inner)
        out[:, columns] = dot(hidden[...], part, ((1,), (1,))).astype(BF16)
        leaving.append(start_copy(out.at[:, columns], produced.at[:, columns], sems, used))
    return leaving


def expert_kernel(side, rows, weights, produced, passed, x, gate, up, down, hidden, out, sems, *, wide, shard):
    members = weights.shape[0]
    inner = weights.shape[2]
    used = []
    mine = side[0]

    def fetch(p, target, first):
        return [
            start_copy(
                weights.at[:, (2 * s + p) * shard : (2 * s + p + 1) * shard, first : first + wide],
                target.at[
                    pl.ds((mine if s == 0 else 1 - mine) * members, members), :, first : first + wide
                ],
                sems,
                used,
            )
            for s in range(2)
        ]

    arrival = start_copy(rows, x, sems, used)
    blocks = []
    for first in range(0, inner, wide):
        blocks.append(fetch(0, gate, first) + fetch(1, up, first))
    last = start_copy(weights.at[:, 4 * shard : 5 * shard, :], down, sems, used)
    arrival.wait()
    for n, first in enumerate(range(0, inner, wide)):
        columns = slice(first, first + wide)
        for copy in blocks[n]:
            copy.wait()
        gated = dot(x[...], gate[:, :, columns].reshape(2 * members * shard, wide))
        upward = dot(x[...], up[:, :, columns].reshape(2 * members * shard, wide))
        hidden[:, columns] = (gated / (1.0 + jnp.exp(-gated)) * upward).astype(BF16)
    leaving = [start_copy(hidden, passed, sems, used)]
    last.wait()
    leaving += project(hidden, down, out, produced, sems, used, wide)
    for copy in leaving:
        copy.wait()


def down_kernel(passed, weights, produced, down, hidden, out, sems, *, wide):
    used = []
    arrivals = [start_copy(passed, hidden, sems, used), start_copy(weights, down, sems, used)]
    for copy in arrivals:
        copy.wait()
    for copy in project(hidden, down, out, produced, sems, used, wide):
        copy.wait()


def combine_kernel(factors, returned, *rest):
    mixture = rest[-1]
    count = mixture.shape[0]
    sums = dot(factors[...], returned[...])
    mixture[...] = (sums[:count] + sums[count:]).astype(BF16)


def per_device(tokens, routes, gate_values, gate_weight, up_weight, down_weight):
    groups = lax.axis_size("expert")
    shards = lax.axis_size("dp")
    count, features = tokens.shape
    top = routes.shape[1]
    capacity = 2 * count * top // groups
    slots = groups * capacity
    _, shard, inner = gate_weight.shape
    half = shards // 2
    joined = jnp.concatenate([gate_weight[0], up_weight[0], down_weight[0].T], axis=0)
    swap = [(d, (d + half) % shards) for d in range(shards)]
    other = lax.ppermute(joined, "dp", swap)
    outgoing, factors = pl.pallas_call(
        lambda *refs: dispatch_kernel(*refs, capacity=capacity),
        out_shape=(
            jax.ShapeDtypeStruct((slots, features), BF16),
            jax.ShapeDtypeStruct((2 * count, slots), BF16),
        ),
        name="dispatch",
    )(routes.T, gate_values.T, tokens)
    other, outgoing = lax.optimization_barrier((other, outgoing))
    sides = [list(range(half)), list(range(half, shards))]
    side = (lax.axis_index("dp") // half).astype(jnp.int32)
    own_down, other_down = joined[2 * shard :], other[2 * shard :]
    first_down = jnp.where(side == 0, own_down, other_down)
    second_down = jnp.where(side == 0, other_down, own_down)
    early = jnp.concatenate([joined[: 2 * shard], other[: 2 * shard], first_down], axis=0)
    weights = lax.all_gather(early, "dp", axis=0, axis_index_groups=sides)
    late = lax.all_gather(second_down, "dp", axis=0, axis_index_groups=sides)

    def exchange(rows, name):
        with jax.named_scope(name):
            blocks = rows.reshape(groups, capacity, rows.shape[1])
            moved = lax.all_to_all(blocks, "expert", split_axis=0, concat_axis=0, tiled=True)
            return moved.reshape(rows.shape)

    arrived = exchange(outgoing, "outward")
    wide = 256
    blocks = inner // wide
    part = features // 2
    anywhere = pl.BlockSpec(memory_space=pl.ANY)
    produced, passed = pl.pallas_call(
        lambda *refs: expert_kernel(*refs, wide=wide, shard=shard),
        out_shape=(
            jax.ShapeDtypeStruct((slots, part), BF16),
            jax.ShapeDtypeStruct((slots, inner), BF16),
        ),
        in_specs=[pl.BlockSpec(memory_space=pltpu.SMEM), anywhere, anywhere],
        out_specs=(anywhere, anywhere),
        scratch_shapes=[
            pltpu.VMEM((slots, features), BF16),
            pltpu.VMEM((shards, shard, inner), BF16),
            pltpu.VMEM((shards, shard, inner), BF16),
            pltpu.VMEM((half, shard, inner), BF16),
            pltpu.VMEM((slots, inner), BF16),
            pltpu.VMEM((slots, part), BF16),
            pltpu.SemaphoreType.DMA((3 + 4 * blocks + part // wide,)),
        ],
        name="expert",
    )(side.reshape(1), arrived, weights)
    first = exchange(produced, "first")
    with jax.named_scope("rest"):
        produced = pl.pallas_call(
            lambda *refs: down_kernel(*refs, wide=wide),
            out_shape=jax.ShapeDtypeStruct((slots, part), BF16),
            in_specs=[anywhere, anywhere],
            out_specs=anywhere,
            scratch_shapes=[
                pltpu.VMEM((half, shard, inner), BF16),
                pltpu.VMEM((slots, inner), BF16),
                pltpu.VMEM((slots, part), BF16),
                pltpu.SemaphoreType.DMA((2 + part // wide,)),
            ],
            name="down",
        )(passed, late)
    second = exchange(produced, "second")
    whole = pl.BlockSpec((2 * count, slots), lambda i: (0, 0))
    rows = pl.BlockSpec((slots, part), lambda i: (0, 0))
    mixture = pl.pallas_call(
        combine_kernel,
        out_shape=jax.ShapeDtypeStruct((count, features), BF16),
        grid=(1,),
        in_specs=[whole, rows],
        out_specs=pl.BlockSpec((count, part), lambda i: (0, 0)),
        name="combine_first",
    )(factors, first)
    return pl.pallas_call(
        combine_kernel,
        out_shape=jax.ShapeDtypeStruct((count, features), BF16),
        grid=(1,),
        in_specs=[whole, rows, anywhere],
        out_specs=pl.BlockSpec((count, part), lambda i: (0, 1)),
        input_output_aliases={2: 0},
        name="combine_second",
    )(factors, second, mixture)


def solution(mesh):
    placed = (
        P(("dp", "expert"), None),
        P(("dp", "expert"), None),
        P(("dp", "expert"), None),
        P("expert", "dp", None),
        P("expert", "dp", None),
        P("expert", None, "dp"),
    )
    return jax.shard_map(
        per_device, mesh=mesh, in_specs=placed, out_specs=P(("dp", "expert"), None), check_vma=False
    )
```

time: 177 us -> 179 us (1.011)
  waiting for transfers between devices: 21 us -> 105 us
  blocking collectives: 59.8 us -> 0 us
  starting transfers between devices: 55.2 us -> 33.9 us
  local copies, waits for them, and re-layouts: 6.29 us -> 1 us
  Pallas kernels: 16.6 us -> 20 us
    all_to_all x1 -> x3, waiting for transfers between devices: 0.01 us -> 75.9 us  [exchange(): lax.all_to_all(blocks, 'expert', split_axis=0, concat_axis=0, tiled=True)]
    all_to_all x1 -> x0, blocking collectives: 59.8 us -> none  [exchange(): lax.all_to_all(blocks, 'expert', split_axis=0, concat_axis=0, tiled=True)]
    ppermute x8 -> x0, starting transfers between devices: 39.3 us -> none  [the longest x3 20.5 us: per_device(): behind.append(lax.ppermute(behind[-1], 'dp', along(-1)))]
    all_gather x1 -> x2, waiting for transfers between devices: 0.01 us -> 28.1 us  [the longest x1 25.4 us: per_device(): late = lax.all_gather(second_down, 'dp', axis=0, axis_index_groups=sides)]
    ppermute x8 -> x0, waiting for transfers between devices: 21 us -> none  [the longest x4 15.2 us: per_device(): ahead.append(lax.ppermute(ahead[-1], 'dp', along(1)))]
    all_to_all x1 -> x3, starting transfers between devices: 11.8 us -> 29.9 us  [exchange(): lax.all_to_all(blocks, 'expert', split_axis=0, concat_axis=0, tiled=True)]
    unnamed x10 -> x6, local copies, waits for them, and re-layouts: 5.57 us -> 0.99 us
    another operation x4 -> x0, other arithmetic: 2.41 us -> none  [the longest x2 1.74 us: per_device(): both = jnp.stack([joined[:2 * shard], other[:2 * shard]])]
  transfers between devices with their start and end apart: 11 -> 6, of which waited for: 7 -> 5; matrix products, arithmetic and copies ran while one was open for 4% -> 0% of each run, Pallas kernels for 2% -> 10%
where the time goes in v4:
time: 179 us; the launch traced here: 178 us
  waiting for transfers between devices  105 us (59%)
  starting transfers between devices  33.9 us (19%)
  Pallas kernels  20 us (11%)
  between operations  13.5 us (8%)
  other arithmetic  4.31 us (2%)
    all_to_all x3, waiting for transfers between devices, exchange(): lax.all_to_all(blocks, 'expert', split_axis=0, concat_axis=0, tiled=True)  75.9 us
    all_to_all x3, starting transfers between devices, exchange(): lax.all_to_all(blocks, 'expert', split_axis=0, concat_axis=0, tiled=True)  29.9 us
    all_gather x1, waiting for transfers between devices, per_device(): late = lax.all_gather(second_down, 'dp', axis=0, axis_index_groups=sides)  25.4 us
    pallas_call x1, Pallas kernels, per_device(): pl.pallas_call(lambda *refs: expert_kernel(*refs, wide=wide, shard=shard)...  8.07 us
    pallas_call x2, Pallas kernels, per_device(): pl.pallas_call(combine_kernel, out_shape=jax.ShapeDtypeStruct((count, fea...  4.91 us
    ppermute x1, starting transfers between devices, per_device(): other = lax.ppermute(joined, 'dp', swap)  4.02 us
    pallas_call x1, Pallas kernels, per_device(): pl.pallas_call(lambda *refs: down_kernel(*refs, wide=wide), out_shape=jax...  3.65 us
  transfers between devices with their start and end apart: 6, of which 5 were waited for; matrix products, arithmetic and copies ran while one was open for 0% of the time, Pallas kernels for 10%

profile of v4, /device:TPU:1, one launch (start us, length us, event | category | flops | bytes accessed | tf_op | source)
XLA Modules:
  0.0 178.2 jit_solution(8138151909375697051)
XLA Ops:
  6.5 0.0 all-gather.5.cloned.1.call-start
  6.5 1.0 pad_maximum_fusion.1
  7.5 4.0 %collective-permute-start = (bf16[192,768]{1,0:T(8,128)(2,1)S(1)}, bf16[192,768]{1,0:T(8,128)(2,1)S(1)}, u32[]{:S(2)}, u32[]{:S(2)}) collective-permute-start(bf16[192,768]{1,0:T(8,128)(2,1)S(1)} %pad_maximum_fusion.1), channel_id=1, source_target_pairs={{0,256},{16,272},{32,288},{48,304},{64,320},{80,336},{96,352},{112... | collective-permute-start | bytes 884744 | tf_op jit(solution)/shard_map/ppermute | solution.py:126
  11.6 3.4 %dispatch.1 = (bf16[512,2048]{1,0:T(8,128)(2,1)}, bf16[256,512]{1,0:T(8,128)(2,1)}) custom-call(s32[2,128]{1,0:T(2,128)} %bitcast.31, f32[2,128]{1,0:T(2,128)} %bitcast.32, bf16[128,2048]{1,0:T(8,128)(2,1)} %refs_2_.1), custom_call_target="tpu_custom_call" | custom-call | tf_op jit(solution)/shard_map/dispatch/pallas_call | solution.py:127
  15.0 0.7 collective-permute-done
  15.7 1.5 broadcast_select_fusion
  17.2 1.8 pad_maximum_fusion
  19.0 0.0 all-gather.5.cloned.1.call-update
  19.0 11.9 %all-to-all-start = ((bf16[16,32,2048]{2,1,0:T(8,128)(2,1)}), bf16[16,32,2048]{2,1,0:T(8,128)(2,1)S(1)}, u32[]{:S(2)}, u32[]{:S(2)}) async-start(bf16[16,32,2048]{2,1,0:T(8,128)(2,1)} %bitcast.23), calls=%async_computation | async-start | bytes 4194304 | tf_op jit(solution)/shard_map/outward/all_to_all | solution.py:148
  30.9 0.0 all-gather.7.cloned.1.call-start
  30.9 0.7 all-gather.7.cloned.1.call-update
  31.7 50.0 %all-to-all-done = bf16[16,32,2048]{2,1,0:T(8,128)(2,1)S(1)} async-done(((bf16[16,32,2048]{2,1,0:T(8,128)(2,1)}), bf16[16,32,2048]{2,1,0:T(8,128)(2,1)S(1)}, u32[]{:S(2)}, u32[]{:S(2)}) %all-to-all-start) | async-done | bytes 2097184 | tf_op jit(solution)/shard_map/outward/all_to_all | solution.py:148
  81.7 2.7 %all-gather.5.cloned.1.call-done = bf16[5120,768]{1,0:T(8,128)(2,1)} async-done(((bf16[320,768]{1,0:T(8,128)(2,1)}), bf16[5120,768]{1,0:T(8,128)(2,1)}) %all-gather.5.cloned.1.call-update) | async-done | bytes 7864336 | tf_op jit(solution)/shard_map/all_gather | solution.py:142
  84.4 8.1 %expert.1 = (bf16[512,1024]{1,0:T(8,128)(2,1)}, bf16[512,768]{1,0:T(8,128)(2,1)}) custom-call(s32[1]{0:T(128)} %bitcast.2.refs_0_, bf16[512,2048]{1,0:T(8,128)(2,1)} %bitcast.18, bf16[16,320,768]{2,1,0:T(8,128)(2,1)} %bitcast.19), custom_call_target="tpu_custom_call" | custom-call | tf_op jit(solution)/shard_map/expert/pallas_call | solution.py:156
  92.5 9.0 %all-to-all-start.2 = ((bf16[16,32,1024]{2,1,0:T(8,128)(2,1)}), bf16[16,32,1024]{2,1,0:T(8,128)(2,1)S(1)}, u32[]{:S(2)}, u32[]{:S(2)}) async-start(bf16[16,32,1024]{2,1,0:T(8,128)(2,1)} %bitcast.25), calls=%async_computation.2 | async-start | bytes 2097152 | tf_op jit(solution)/shard_map/first/all_to_all | solution.py:148
  101.5 25.4 %all-gather.7.cloned.1.call-done = bf16[1024,768]{1,0:T(8,128)(2,1)} async-done(((bf16[64,768]{1,0:T(8,128)(2,1)}), bf16[1024,768]{1,0:T(8,128)(2,1)}) %all-gather.7.cloned.1.call-update) | async-done | bytes 1572880 | tf_op jit(solution)/shard_map/all_gather | solution.py:143
  126.9 3.7 %down.1 = bf16[512,1024]{1,0:T(8,128)(2,1)} custom-call(bf16[512,768]{1,0:T(8,128)(2,1)} %get-tuple-element.15.refs_0_, bf16[16,64,768]{2,1,0:T(8,128)(2,1)} %bitcast.24), custom_call_target="tpu_custom_call" | custom-call | tf_op jit(solution)/shard_map/rest/down/pallas_call | solution.py:177
  130.6 0.0 all-to-all-done.2
  130.6 0.0 copy-start.1
  130.6 9.0 %all-to-all-start.1 = ((bf16[16,32,1024]{2,1,0:T(8,128)(2,1)}), bf16[16,32,1024]{2,1,0:T(8,128)(2,1)S(1)}, u32[]{:S(2)}, u32[]{:S(2)}) async-start(bf16[16,32,1024]{2,1,0:T(8,128)(2,1)} %bitcast.21), calls=%async_computation.1 | async-start | bytes 2097152 | tf_op jit(solution)/shard_map/second/all_to_all | solution.py:148
  139.6 2.5 %combine_first.1.rest_0_ = bf16[128,2048]{1,0:T(8,128)(2,1)} custom-call(bf16[256,512]{1,0:T(8,128)(2,1)} %get-tuple-element.11.factors, bf16[512,1024]{1,0:T(8,128)(2,1)} %bitcast.20), custom_call_target="tpu_custom_call" | custom-call | tf_op jit(solution)/shard_map/combine_first/pallas_call | solution.py:193
  142.0 25.8 %all-to-all-done.1 = bf16[16,32,1024]{2,1,0:T(8,128)(2,1)S(1)} async-done(((bf16[16,32,1024]{2,1,0:T(8,128)(2,1)}), bf16[16,32,1024]{2,1,0:T(8,128)(2,1)S(1)}, u32[]{:S(2)}, u32[]{:S(2)}) %all-to-all-start.1) | async-done | bytes 1048608 | tf_op jit(solution)/shard_map/second/all_to_all | solution.py:148
  167.9 1.0 copy-done.2
  168.9 2.5 %combine_second.1 = bf16[128,2048]{1,0:T(8,128)(2,1)} custom-call(bf16[256,512]{1,0:T(8,128)(2,1)} %get-tuple-element.11.factors, bf16[512,1024]{1,0:T(8,128)(2,1)} %bitcast.22, bf16[128,2048]{1,0:T(8,128)(2,1)} %combine_first.1.rest_0_), custom_call_target="tpu_custom_call", output_to_operand_aliasing={{}: (2, {})} | custom-call | tf_op jit(solution)/shard_map/combine_second/pallas_call | solution.py:201
  (5 shorter events, 0.0 us)
Async XLA Ops:
  6.5 77.8 %all-gather.5.cloned.1.call-start = ((), (), s32[]{:S(2)}) async-start(), calls=%async_computation.3 | async-start | bytes 8355840 | tf_op jit(solution)/shard_map/all_gather | solution.py:142
  7.5 8.1 %collective-permute-start = (bf16[192,768]{1,0:T(8,128)(2,1)S(1)}, bf16[192,768]{1,0:T(8,128)(2,1)S(1)}, u32[]{:S(2)}, u32[]{:S(2)}) collective-permute-start(bf16[192,768]{1,0:T(8,128)(2,1)S(1)} %pad_maximum_fusion.1), channel_id=1, source_target_pairs={{0,256},{16,272},{32,288},{48,304},{64,320},{80,336},{96,352},{112... | collective-permute-start | bytes 884744 | tf_op jit(solution)/shard_map/ppermute | solution.py:126
  19.0 62.6 %all-to-all-start = ((bf16[16,32,2048]{2,1,0:T(8,128)(2,1)}), bf16[16,32,2048]{2,1,0:T(8,128)(2,1)S(1)}, u32[]{:S(2)}, u32[]{:S(2)}) async-start(bf16[16,32,2048]{2,1,0:T(8,128)(2,1)} %bitcast.23), calls=%async_computation | async-start | bytes 4194304 | tf_op jit(solution)/shard_map/outward/all_to_all | solution.py:148
  30.9 96.0 %all-gather.7.cloned.1.call-start = ((), (), s32[]{:S(2)}) async-start(), calls=%async_computation.4 | async-start | bytes 1671168 | tf_op jit(solution)/shard_map/all_gather | solution.py:143
  81.7 2.7 %copy-start = (bf16[16,32,2048]{2,1,0:T(8,128)(2,1)}, bf16[16,32,2048]{2,1,0:T(8,128)(2,1)S(1)}, u32[]{:S(2)}) copy-start(bf16[16,32,2048]{2,1,0:T(8,128)(2,1)S(1)} %all-to-all-done) | copy-start | bytes 6291460
  92.5 38.1 %all-to-all-start.2 = ((bf16[16,32,1024]{2,1,0:T(8,128)(2,1)}), bf16[16,32,1024]{2,1,0:T(8,128)(2,1)S(1)}, u32[]{:S(2)}, u32[]{:S(2)}) async-start(bf16[16,32,1024]{2,1,0:T(8,128)(2,1)} %bitcast.25), calls=%async_computation.2 | async-start | bytes 2097152 | tf_op jit(solution)/shard_map/first/all_to_all | solution.py:148
  130.6 9.0 %copy-start.1 = (bf16[16,32,1024]{2,1,0:T(8,128)(2,1)}, bf16[16,32,1024]{2,1,0:T(8,128)(2,1)S(1)}, u32[]{:S(2)}) copy-start(bf16[16,32,1024]{2,1,0:T(8,128)(2,1)S(1)} %all-to-all-done.2) | copy-start | bytes 3145732
  130.6 37.3 %all-to-all-start.1 = ((bf16[16,32,1024]{2,1,0:T(8,128)(2,1)}), bf16[16,32,1024]{2,1,0:T(8,128)(2,1)S(1)}, u32[]{:S(2)}, u32[]{:S(2)}) async-start(bf16[16,32,1024]{2,1,0:T(8,128)(2,1)} %bitcast.21), calls=%async_computation.1 | async-start | bytes 2097152 | tf_op jit(solution)/shard_map/second/all_to_all | solution.py:148
  167.9 1.0 copy-start.2
Sparse Core Ops, SparseCore 0:
  19.1 65.1 all-gather.4
  86.5 40.3 all-gather.6

commit v5 on v2

--- a/solution.py
+++ b/solution.py
@@ -13,7 +13,7 @@
     return lax.dot_general(a, b, (dims, ((), ())), preferred_element_type=F32)
 
 
-def dispatch_kernel(routes, gates, tokens, outgoing, high, low, *, capacity):
+def dispatch_kernel(routes, gates, tokens, outgoing, factors, *, capacity):
     slots = outgoing.shape[0]
     count = tokens.shape[0]
     top = routes.shape[0]
@@ -34,8 +34,8 @@
     outgoing[...] = dot(chosen.astype(BF16), tokens[...]).astype(BF16)
     weight = jnp.transpose(chosen * weight)
     rounded = weight.astype(BF16)
-    high[...] = rounded
-    low[...] = (weight - rounded.astype(F32)).astype(BF16)
+    factors[:count, :] = rounded
+    factors[count:, :] = (weight - rounded.astype(F32)).astype(BF16)
 
 
 def expert_kernel(side, rows, weights, produced, x, gate, up, down, hidden, out, sems, *, wide, shard):
@@ -88,9 +88,10 @@
         copy.wait()
 
 
-def combine_kernel(high, low, returned, mixture):
-    rows = returned[...]
-    mixture[...] = (dot(high[...], rows) + dot(low[...], rows)).astype(BF16)
+def combine_kernel(factors, returned, mixture):
+    count = mixture.shape[0]
+    sums = dot(factors[...], returned[...])
+    mixture[...] = (sums[:count] + sums[count:]).astype(BF16)
 
 
 def per_device(tokens, routes, gate_values, gate_weight, up_weight, down_weight):
@@ -101,22 +102,23 @@
     capacity = 2 * count * top // groups
     slots = groups * capacity
     _, shard, inner = gate_weight.shape
+    half = shards // 2
     joined = jnp.concatenate([gate_weight[0], up_weight[0], down_weight[0].T], axis=0)
-    half = shards // 2
     swap = [(d, (d + half) % shards) for d in range(shards)]
-    both = jnp.stack([joined, lax.ppermute(joined, "dp", swap)])
-    sides = [list(range(half)), list(range(half, shards))]
-    weights = lax.all_gather(both, "dp", axis=0, axis_index_groups=sides)
-    side = (lax.axis_index("dp") // half).astype(jnp.int32).reshape(1)
-    outgoing, high, low = pl.pallas_call(
+    other = lax.ppermute(joined, "dp", swap)
+    outgoing, factors = pl.pallas_call(
         lambda *refs: dispatch_kernel(*refs, capacity=capacity),
         out_shape=(
             jax.ShapeDtypeStruct((slots, features), BF16),
-            jax.ShapeDtypeStruct((count, slots), BF16),
-            jax.ShapeDtypeStruct((count, slots), BF16),
+            jax.ShapeDtypeStruct((2 * count, slots), BF16),
         ),
         name="dispatch",
     )(routes.T, gate_values.T, tokens)
+    other, outgoing = lax.optimization_barrier((other, outgoing))
+    sides = [list(range(half)), list(range(half, shards))]
+    both = jnp.stack([joined, other])
+    weights = lax.all_gather(both, "dp", axis=0, axis_index_groups=sides)
+    side = (lax.axis_index("dp") // half).astype(jnp.int32).reshape(1)
 
     def exchange(rows):
         blocks = rows.reshape(groups, capacity, features)
@@ -125,6 +127,8 @@
 
     arrived = exchange(outgoing)
     wide = 256
+    anywhere = pl.BlockSpec(memory_space=pl.ANY)
+    blocks = inner // wide
     anywhere = pl.BlockSpec(memory_space=pl.ANY)
     blocks = inner // wide
     produced = pl.pallas_call(
@@ -144,19 +148,11 @@
         name="expert",
     )(side, arrived, weights)
     returned = exchange(produced)
-    band = 512
     return pl.pallas_call(
         combine_kernel,
         out_shape=jax.ShapeDtypeStruct((count, features), BF16),
-        grid=(features // band,),
-        in_specs=[
-            pl.BlockSpec((count, slots), lambda i: (0, 0)),
-            pl.BlockSpec((count, slots), lambda i: (0, 0)),
-            pl.BlockSpec((slots, band), lambda i: (0, i)),
-        ],
-        out_specs=pl.BlockSpec((count, band), lambda i: (0, i)),
         name="combine",
-    )(high, low, returned)
+    )(factors, returned)
 
 
 def solution(mesh):

time: 169 us -> 168 us (level)
    ppermute x1, waiting for transfers between devices: 4.1 us -> 0.81 us  [per_device(): other = lax.ppermute(joined, 'dp', swap)]
    all_gather x1, waiting for transfers between devices: 6.87 us -> 10.1 us  [per_device(): weights = lax.all_gather(both, 'dp', axis=0, axis_index_groups=sides)]
where the time goes in v5:
time: 168 us
  waiting for transfers between devices  61.7 us (37%)
  blocking collectives  59.5 us (35%)
  starting transfers between devices  15.9 us (9%)
  Pallas kernels  15.5 us (9%)
  between operations  13.4 us (8%)
  other arithmetic  1.9 us (1%)
    all_to_all x1, blocking collectives, exchange(): lax.all_to_all(blocks, 'expert', split_axis=0, concat_axis=0, tiled=True)  59.5 us
    all_to_all x1, waiting for transfers between devices, exchange(): lax.all_to_all(blocks, 'expert', split_axis=0, concat_axis=0, tiled=True)  50.8 us
    all_to_all x1, starting transfers between devices, exchange(): lax.all_to_all(blocks, 'expert', split_axis=0, concat_axis=0, tiled=True)  11.9 us
    all_gather x1, waiting for transfers between devices, per_device(): weights = lax.all_gather(both, 'dp', axis=0, axis_index_groups=sides)  10.1 us
    pallas_call x1, Pallas kernels, per_device(): pl.pallas_call(lambda *refs: expert_kernel(*refs, wide=wide, shard=shard)...  9 us
    ppermute x1, starting transfers between devices, per_device(): other = lax.ppermute(joined, 'dp', swap)  4.02 us
  transfers between devices with their start and end apart: 3, of which 3 were waited for; matrix products, arithmetic and copies ran while one was open for 0% of the time, Pallas kernels for 2%

profile of v5, /device:TPU:1, one launch (start us, length us, event | category | flops | bytes accessed | tf_op | source)
XLA Modules:
  0.0 167.9 jit_solution(13165055370572802035)
XLA Ops:
  6.5 0.0 all-gather.3.cloned.1.call-start
  6.5 1.0 fusion
  7.6 4.0 %collective-permute-start = (bf16[192,768]{1,0:T(8,128)(2,1)S(1)}, bf16[192,768]{1,0:T(8,128)(2,1)S(1)}, u32[]{:S(2)}, u32[]{:S(2)}) collective-permute-start(bf16[192,768]{1,0:T(8,128)(2,1)S(1)} %get-tuple-element.14), channel_id=1, source_target_pairs={{0,256},{16,272},{32,288},{48,304},{64,320},{80,336},{96,352},{112... | collective-permute-start | bytes 884744 | tf_op jit(solution)/shard_map/ppermute | solution.py:108
  11.6 3.3 %dispatch.1 = (bf16[512,2048]{1,0:T(8,128)(2,1)}, bf16[256,512]{1,0:T(8,128)(2,1)}) custom-call(s32[2,128]{1,0:T(2,128)} %bitcast.25, f32[2,128]{1,0:T(2,128)} %bitcast.26, bf16[128,2048]{1,0:T(8,128)(2,1)} %refs_2_.1), custom_call_target="tpu_custom_call" | custom-call | tf_op jit(solution)/shard_map/dispatch/pallas_call | solution.py:109
  14.9 0.8 collective-permute-done
  15.7 0.9 pad_maximum_fusion
  16.6 0.0 all-gather.3.cloned.1.call-update
  16.6 11.9 %all-to-all-start = ((bf16[16,32,2048]{2,1,0:T(8,128)(2,1)}), bf16[16,32,2048]{2,1,0:T(8,128)(2,1)S(1)}, u32[]{:S(2)}, u32[]{:S(2)}) async-start(bf16[16,32,2048]{2,1,0:T(8,128)(2,1)} %bitcast.20), calls=%async_computation | async-start | bytes 4194304 | tf_op jit(solution)/shard_map/all_to_all | solution.py:125
  28.5 50.8 %all-to-all-done = bf16[16,32,2048]{2,1,0:T(8,128)(2,1)S(1)} async-done(((bf16[16,32,2048]{2,1,0:T(8,128)(2,1)}), bf16[16,32,2048]{2,1,0:T(8,128)(2,1)S(1)}, u32[]{:S(2)}, u32[]{:S(2)}) %all-to-all-start) | async-done | bytes 2097184 | tf_op jit(solution)/shard_map/all_to_all | solution.py:125
  79.2 0.0 copy-start
  79.2 10.1 %all-gather.3.cloned.1.call-done = bf16[32,192,768]{2,1,0:T(8,128)(2,1)} async-done(((bf16[2,192,768]{2,1,0:T(8,128)(2,1)}), bf16[32,192,768]{2,1,0:T(8,128)(2,1)}) %all-gather.3.cloned.1.call-update) | async-done | bytes 9437200 | tf_op jit(solution)/shard_map/all_gather | solution.py:120
  89.4 0.0 copy-done
  89.4 9.0 %expert.1 = bf16[512,2048]{1,0:T(8,128)(2,1)} custom-call(s32[1]{0:T(128)} %bitcast.2.refs_0_, bf16[512,2048]{1,0:T(8,128)(2,1)} %bitcast.18, bf16[16,2,192,768]{3,2,1,0:T(8,128)(2,1)} %bitcast.16), custom_call_target="tpu_custom_call" | custom-call | tf_op jit(solution)/shard_map/expert/pallas_call | solution.py:134
  98.4 59.5 %all_to_all.10 = bf16[16,32,2048]{2,1,0:T(8,128)(2,1)} all-to-all(bf16[16,32,2048]{2,1,0:T(8,128)(2,1)} %bitcast.19), channel_id=1, replica_groups=mesh['dp'=32,'expert'=16] {'expert'}, dimensions={0} | all-to-all | bytes 4194304 | tf_op jit(solution)/shard_map/all_to_all | solution.py:125
  157.9 3.2 %combine.1 = bf16[128,2048]{1,0:T(8,128)(2,1)} custom-call(bf16[256,512]{1,0:T(8,128)(2,1)} %get-tuple-element.9.factors, bf16[512,2048]{1,0:T(8,128)(2,1)} %bitcast.17), custom_call_target="tpu_custom_call" | custom-call | tf_op jit(solution)/shard_map/combine/pallas_call | solution.py:151
Async XLA Ops:
  6.5 82.8 %all-gather.3.cloned.1.call-start = ((), (), s32[]{:S(2)}) async-start(), calls=%async_computation.2 | async-start | bytes 10027008 | tf_op jit(solution)/shard_map/all_gather | solution.py:120
  7.6 8.1 %collective-permute-start = (bf16[192,768]{1,0:T(8,128)(2,1)S(1)}, bf16[192,768]{1,0:T(8,128)(2,1)S(1)}, u32[]{:S(2)}, u32[]{:S(2)}) collective-permute-start(bf16[192,768]{1,0:T(8,128)(2,1)S(1)} %get-tuple-element.14), channel_id=1, source_target_pairs={{0,256},{16,272},{32,288},{48,304},{64,320},{80,336},{96,352},{112... | collective-permute-start | bytes 884744 | tf_op jit(solution)/shard_map/ppermute | solution.py:108
  16.6 62.6 %all-to-all-start = ((bf16[16,32,2048]{2,1,0:T(8,128)(2,1)}), bf16[16,32,2048]{2,1,0:T(8,128)(2,1)S(1)}, u32[]{:S(2)}, u32[]{:S(2)}) async-start(bf16[16,32,2048]{2,1,0:T(8,128)(2,1)} %bitcast.20), calls=%async_computation | async-start | bytes 4194304 | tf_op jit(solution)/shard_map/all_to_all | solution.py:125
  79.2 10.1 %copy-start = (bf16[16,32,2048]{2,1,0:T(8,128)(2,1)}, bf16[16,32,2048]{2,1,0:T(8,128)(2,1)S(1)}, u32[]{:S(2)}) copy-start(bf16[16,32,2048]{2,1,0:T(8,128)(2,1)S(1)} %all-to-all-done) | copy-start | bytes 6291460
Sparse Core Ops, SparseCore 0:
  16.7 72.5 all-gather.2

commit v6 on v5

--- a/solution.py
+++ b/solution.py
@@ -120,9 +120,25 @@
     weights = lax.all_gather(both, "dp", axis=0, axis_index_groups=sides)
     side = (lax.axis_index("dp") // half).astype(jnp.int32).reshape(1)
 
+    circles = [
+        [
+            ((b if e < groups // 2 else 1 - b) * half + i) * groups + e
+            for e in range(groups)
+        ]
+        for b in range(2)
+        for i in range(half)
+    ]
+
     def exchange(rows):
         blocks = rows.reshape(groups, capacity, features)
-        moved = lax.all_to_all(blocks, "expert", split_axis=0, concat_axis=0, tiled=True)
+        moved = lax.all_to_all(
+            blocks,
+            ("dp", "expert"),
+            split_axis=0,
+            concat_axis=0,
+            tiled=True,
+            axis_index_groups=circles,
+        )
         return moved.reshape(slots, features)
 
     arrived = exchange(outgoing)

time: 168 us -> 166 us (0.988)
  blocking collectives: 59.5 us -> 57.3 us
    all_gather x1, waiting for transfers between devices: 10.1 us -> 13.3 us  [per_device(): weights = lax.all_gather(both, 'dp', axis=0, axis_index_groups=sides)]
    all_to_all x1, waiting for transfers between devices: 50.8 us -> 48.3 us  [exchange(): lax.all_to_all(blocks, ('dp', 'expert'), split_axis=0, concat_axis=0, til...]
    all_to_all x1, blocking collectives: 59.5 us -> 57.3 us  [exchange(): lax.all_to_all(blocks, ('dp', 'expert'), split_axis=0, concat_axis=0, til...]
where the time goes in v6:
time: 166 us
  waiting for transfers between devices  62.5 us (38%)
  blocking collectives  57.3 us (35%)
  Pallas kernels  15.5 us (9%)
  starting transfers between devices  15.1 us (9%)
  between operations  13.4 us (8%)
  other arithmetic  1.9 us (1%)
    all_to_all x1, blocking collectives, exchange(): lax.all_to_all(blocks, ('dp', 'expert'), split_axis=0, concat_axis=0, til...  57.3 us
    all_to_all x1, waiting for transfers between devices, exchange(): lax.all_to_all(blocks, ('dp', 'expert'), split_axis=0, concat_axis=0, til...  48.3 us
    all_gather x1, waiting for transfers between devices, per_device(): weights = lax.all_gather(both, 'dp', axis=0, axis_index_groups=sides)  13.3 us
    all_to_all x1, starting transfers between devices, exchange(): lax.all_to_all(blocks, ('dp', 'expert'), split_axis=0, concat_axis=0, til...  11.1 us
    pallas_call x1, Pallas kernels, per_device(): pl.pallas_call(lambda *refs: expert_kernel(*refs, wide=wide, shard=shard)...  9 us
    ppermute x1, starting transfers between devices, per_device(): other = lax.ppermute(joined, 'dp', swap)  4.02 us
  transfers between devices with their start and end apart: 3, of which 3 were waited for; matrix products, arithmetic and copies ran while one was open for 0% of the time, Pallas kernels for 2%

profile of v6, /device:TPU:1, one launch (start us, length us, event | category | flops | bytes accessed | tf_op | source)
XLA Modules:
  0.0 165.8 jit_solution(12642798293361376386)
XLA Ops:
  6.5 0.0 all-gather.3.cloned.1.call-start
  6.5 1.0 fusion
  7.6 4.0 %collective-permute-start = (bf16[192,768]{1,0:T(8,128)(2,1)S(1)}, bf16[192,768]{1,0:T(8,128)(2,1)S(1)}, u32[]{:S(2)}, u32[]{:S(2)}) collective-permute-start(bf16[192,768]{1,0:T(8,128)(2,1)S(1)} %get-tuple-element.14), channel_id=1, source_target_pairs={{0,256},{16,272},{32,288},{48,304},{64,320},{80,336},{96,352},{112... | collective-permute-start | bytes 884744 | tf_op jit(solution)/shard_map/ppermute | solution.py:108
  11.6 3.3 %dispatch.1 = (bf16[512,2048]{1,0:T(8,128)(2,1)}, bf16[256,512]{1,0:T(8,128)(2,1)}) custom-call(s32[2,128]{1,0:T(2,128)} %bitcast.25, f32[2,128]{1,0:T(2,128)} %bitcast.26, bf16[128,2048]{1,0:T(8,128)(2,1)} %refs_2_.1), custom_call_target="tpu_custom_call" | custom-call | tf_op jit(solution)/shard_map/dispatch/pallas_call | solution.py:109
  14.9 0.8 collective-permute-done
  15.7 0.9 pad_maximum_fusion
  16.6 0.0 all-gather.3.cloned.1.call-update
  16.6 11.1 %all-to-all-start = ((bf16[16,32,2048]{2,1,0:T(8,128)(2,1)}), bf16[16,32,2048]{2,1,0:T(8,128)(2,1)S(1)}, u32[]{:S(2)}, u32[]{:S(2)}) async-start(bf16[16,32,2048]{2,1,0:T(8,128)(2,1)} %bitcast.20), calls=%async_computation | async-start | bytes 4194304 | tf_op jit(solution)/shard_map/all_to_all | solution.py:134
  27.7 48.3 %all-to-all-done = bf16[16,32,2048]{2,1,0:T(8,128)(2,1)S(1)} async-done(((bf16[16,32,2048]{2,1,0:T(8,128)(2,1)}), bf16[16,32,2048]{2,1,0:T(8,128)(2,1)S(1)}, u32[]{:S(2)}, u32[]{:S(2)}) %all-to-all-start) | async-done | bytes 2097184 | tf_op jit(solution)/shard_map/all_to_all | solution.py:134
  76.0 0.0 copy-start
  76.1 13.3 %all-gather.3.cloned.1.call-done = bf16[32,192,768]{2,1,0:T(8,128)(2,1)} async-done(((bf16[2,192,768]{2,1,0:T(8,128)(2,1)}), bf16[32,192,768]{2,1,0:T(8,128)(2,1)}) %all-gather.3.cloned.1.call-update) | async-done | bytes 9437200 | tf_op jit(solution)/shard_map/all_gather | solution.py:120
  89.4 0.0 copy-done
  89.4 9.0 %expert.1 = bf16[512,2048]{1,0:T(8,128)(2,1)} custom-call(s32[1]{0:T(128)} %bitcast.2.refs_0_, bf16[512,2048]{1,0:T(8,128)(2,1)} %bitcast.18, bf16[16,2,192,768]{3,2,1,0:T(8,128)(2,1)} %bitcast.16), custom_call_target="tpu_custom_call" | custom-call | tf_op jit(solution)/shard_map/expert/pallas_call | solution.py:150
  98.4 57.3 %all_to_all.10 = bf16[16,32,2048]{2,1,0:T(8,128)(2,1)} all-to-all(bf16[16,32,2048]{2,1,0:T(8,128)(2,1)} %bitcast.19), channel_id=1, replica_groups={{0,1,2,3,4,5,6,7,264,265,266,267,268,269,270,271},{16,17,18,19,20,21,22..., dimensions={0} | all-to-all | bytes 4194304 | tf_op jit(solution)/shard_map/all_to_all | solution.py:134
  155.7 3.2 %combine.1 = bf16[128,2048]{1,0:T(8,128)(2,1)} custom-call(bf16[256,512]{1,0:T(8,128)(2,1)} %get-tuple-element.9.factors, bf16[512,2048]{1,0:T(8,128)(2,1)} %bitcast.17), custom_call_target="tpu_custom_call" | custom-call | tf_op jit(solution)/shard_map/combine/pallas_call | solution.py:167
Async XLA Ops:
  6.5 82.8 %all-gather.3.cloned.1.call-start = ((), (), s32[]{:S(2)}) async-start(), calls=%async_computation.2 | async-start | bytes 10027008 | tf_op jit(solution)/shard_map/all_gather | solution.py:120
  7.6 8.1 %collective-permute-start = (bf16[192,768]{1,0:T(8,128)(2,1)S(1)}, bf16[192,768]{1,0:T(8,128)(2,1)S(1)}, u32[]{:S(2)}, u32[]{:S(2)}) collective-permute-start(bf16[192,768]{1,0:T(8,128)(2,1)S(1)} %get-tuple-element.14), channel_id=1, source_target_pairs={{0,256},{16,272},{32,288},{48,304},{64,320},{80,336},{96,352},{112... | collective-permute-start | bytes 884744 | tf_op jit(solution)/shard_map/ppermute | solution.py:108
  16.6 59.5 %all-to-all-start = ((bf16[16,32,2048]{2,1,0:T(8,128)(2,1)}), bf16[16,32,2048]{2,1,0:T(8,128)(2,1)S(1)}, u32[]{:S(2)}, u32[]{:S(2)}) async-start(bf16[16,32,2048]{2,1,0:T(8,128)(2,1)} %bitcast.20), calls=%async_computation | async-start | bytes 4194304 | tf_op jit(solution)/shard_map/all_to_all | solution.py:134
  76.0 13.3 %copy-start = (bf16[16,32,2048]{2,1,0:T(8,128)(2,1)}, bf16[16,32,2048]{2,1,0:T(8,128)(2,1)S(1)}, u32[]{:S(2)}) copy-start(bf16[16,32,2048]{2,1,0:T(8,128)(2,1)S(1)} %all-to-all-done) | copy-start | bytes 6291460
Sparse Core Ops, SparseCore 0:
  16.7 72.5 all-gather.2

commit v7 on v6

--- a/solution.py
+++ b/solution.py
@@ -51,6 +51,8 @@
         copy.start()
         return copy
 
+    cuts = [(first, wide) for first in range(0, inner, wide)]
+
     def fetch(p, target, first, size):
         return [
             begin(
@@ -64,16 +66,16 @@
 
     arrival = begin(rows, x)
     blocks = []
-    for first in range(0, inner, wide):
-        blocks.append(fetch(0, gate, first, wide) + fetch(1, up, first, wide))
+    for first, size in cuts:
+        blocks.append(fetch(0, gate, first, size) + fetch(1, up, first, size))
     last = fetch(2, down, 0, inner)
     arrival.wait()
-    for n, first in enumerate(range(0, inner, wide)):
-        columns = slice(first, first + wide)
+    for n, (first, size) in enumerate(cuts):
+        columns = slice(first, first + size)
         for copy in blocks[n]:
             copy.wait()
-        gated = dot(x[...], gate[:, :, columns].reshape(2 * members * shard, wide))
-        upward = dot(x[...], up[:, :, columns].reshape(2 * members * shard, wide))
+        gated = dot(x[...], gate[:, :, columns].reshape(2 * members * shard, size))
+        upward = dot(x[...], up[:, :, columns].reshape(2 * members * shard, size))
         hidden[:, columns] = (gated / (1.0 + jnp.exp(-gated)) * upward).astype(BF16)
     for copy in last:
         copy.wait()
@@ -88,10 +90,26 @@
         copy.wait()
 
 
-def combine_kernel(factors, returned, mixture):
-    count = mixture.shape[0]
-    sums = dot(factors[...], returned[...])
-    mixture[...] = (sums[:count] + sums[count:]).astype(BF16)
+def combine_kernel(factors, returned, mixture, rows, out, sems, *, band):
+    count, features = mixture.shape
+    bands = [slice(first, first + band) for first in range(0, features, band)]
+    arriving = []
+    for i, columns in enumerate(bands):
+        copy = pltpu.make_async_copy(returned.at[:, columns], rows.at[:, columns], sems.at[i])
+        copy.start()
+        arriving.append(copy)
+    leaving = []
+    for i, columns in enumerate(bands):
+        arriving[i].wait()
+        sums = dot(factors[...], rows[:, columns])
+        out[:, columns] = (sums[:count] + sums[count:]).astype(BF16)
+        copy = pltpu.make_async_copy(
+            out.at[:, columns], mixture.at[:, columns], sems.at[len(bands) + i]
+        )
+        copy.start()
+        leaving.append(copy)
+    for copy in leaving:
+        copy.wait()
 
 
 def per_device(tokens, routes, gate_values, gate_weight, up_weight, down_weight):
@@ -144,9 +162,7 @@
     arrived = exchange(outgoing)
     wide = 256
     anywhere = pl.BlockSpec(memory_space=pl.ANY)
-    blocks = inner // wide
     anywhere = pl.BlockSpec(memory_space=pl.ANY)
-    blocks = inner // wide
     produced = pl.pallas_call(
         lambda *refs: expert_kernel(*refs, wide=wide, shard=shard),
         out_shape=jax.ShapeDtypeStruct((slots, features), BF16),
@@ -159,14 +175,22 @@
             pltpu.VMEM((shards, shard, inner), BF16),
             pltpu.VMEM((slots, inner), BF16),
             pltpu.VMEM((slots, features), BF16),
-            pltpu.SemaphoreType.DMA((1 + 4 * blocks + 2 + features // wide,)),
+            pltpu.SemaphoreType.DMA((1 + 4 * (inner // wide) + 2 + features // wide,)),
         ],
         name="expert",
     )(side, arrived, weights)
     returned = exchange(produced)
+    band = 512
     return pl.pallas_call(
-        combine_kernel,
+        lambda *refs: combine_kernel(*refs, band=band),
         out_shape=jax.ShapeDtypeStruct((count, features), BF16),
+        in_specs=[pl.BlockSpec(memory_space=pltpu.VMEM), anywhere],
+        out_specs=anywhere,
+        scratch_shapes=[
+            pltpu.VMEM((slots, features), BF16),
+            pltpu.VMEM((count, features), BF16),
+            pltpu.SemaphoreType.DMA((2 * (features // band),)),
+        ],
         name="combine",
     )(factors, returned)
 

time: 166 us -> 167 us (level)
  no operation moved by 1% of the time
where the time goes in v7:
time: 167 us
  waiting for transfers between devices  62.5 us (37%)
  blocking collectives  57.3 us (34%)
  Pallas kernels  16.2 us (10%)
  starting transfers between devices  15.1 us (9%)
  between operations  13.5 us (8%)
  other arithmetic  1.9 us (1%)
    all_to_all x1, blocking collectives, exchange(): lax.all_to_all(blocks, ('dp', 'expert'), split_axis=0, concat_axis=0, til...  57.3 us
    all_to_all x1, waiting for transfers between devices, exchange(): lax.all_to_all(blocks, ('dp', 'expert'), split_axis=0, concat_axis=0, til...  48.3 us
    all_gather x1, waiting for transfers between devices, per_device(): weights = lax.all_gather(both, 'dp', axis=0, axis_index_groups=sides)  13.3 us
    all_to_all x1, starting transfers between devices, exchange(): lax.all_to_all(blocks, ('dp', 'expert'), split_axis=0, concat_axis=0, til...  11.1 us
    pallas_call x1, Pallas kernels, per_device(): pl.pallas_call(lambda *refs: expert_kernel(*refs, wide=wide, shard=shard)...  9 us
    ppermute x1, starting transfers between devices, per_device(): other = lax.ppermute(joined, 'dp', swap)  4.02 us
    pallas_call x1, Pallas kernels, per_device(): pl.pallas_call(lambda *refs: combine_kernel(*refs, band=band), out_shape=...  3.93 us
  transfers between devices with their start and end apart: 3, of which 3 were waited for; matrix products, arithmetic and copies ran while one was open for 0% of the time, Pallas kernels for 2%

profile of v7, /device:TPU:1, one launch (start us, length us, event | category | flops | bytes accessed | tf_op | source)
XLA Modules:
  0.0 166.5 jit_solution(15783325842001017331)
XLA Ops:
  6.5 0.0 all-gather.3.cloned.1.call-start
  6.5 1.0 fusion
  7.6 4.0 %collective-permute-start = (bf16[192,768]{1,0:T(8,128)(2,1)S(1)}, bf16[192,768]{1,0:T(8,128)(2,1)S(1)}, u32[]{:S(2)}, u32[]{:S(2)}) collective-permute-start(bf16[192,768]{1,0:T(8,128)(2,1)S(1)} %get-tuple-element.14), channel_id=1, source_target_pairs={{0,256},{16,272},{32,288},{48,304},{64,320},{80,336},{96,352},{112... | collective-permute-start | bytes 884744 | tf_op jit(solution)/shard_map/ppermute | solution.py:126
  11.6 3.3 %dispatch.1 = (bf16[512,2048]{1,0:T(8,128)(2,1)}, bf16[256,512]{1,0:T(8,128)(2,1)}) custom-call(s32[2,128]{1,0:T(2,128)} %bitcast.25, f32[2,128]{1,0:T(2,128)} %bitcast.26, bf16[128,2048]{1,0:T(8,128)(2,1)} %refs_2_.1), custom_call_target="tpu_custom_call" | custom-call | tf_op jit(solution)/shard_map/dispatch/pallas_call | solution.py:127
  14.9 0.8 collective-permute-done
  15.7 0.9 pad_maximum_fusion
  16.6 0.0 all-gather.3.cloned.1.call-update
  16.6 11.1 %all-to-all-start = ((bf16[16,32,2048]{2,1,0:T(8,128)(2,1)}), bf16[16,32,2048]{2,1,0:T(8,128)(2,1)S(1)}, u32[]{:S(2)}, u32[]{:S(2)}) async-start(bf16[16,32,2048]{2,1,0:T(8,128)(2,1)} %bitcast.20), calls=%async_computation | async-start | bytes 4194304 | tf_op jit(solution)/shard_map/all_to_all | solution.py:152
  27.7 48.3 %all-to-all-done = bf16[16,32,2048]{2,1,0:T(8,128)(2,1)S(1)} async-done(((bf16[16,32,2048]{2,1,0:T(8,128)(2,1)}), bf16[16,32,2048]{2,1,0:T(8,128)(2,1)S(1)}, u32[]{:S(2)}, u32[]{:S(2)}) %all-to-all-start) | async-done | bytes 2097184 | tf_op jit(solution)/shard_map/all_to_all | solution.py:152
  76.0 0.0 copy-start
  76.1 13.3 %all-gather.3.cloned.1.call-done = bf16[32,192,768]{2,1,0:T(8,128)(2,1)} async-done(((bf16[2,192,768]{2,1,0:T(8,128)(2,1)}), bf16[32,192,768]{2,1,0:T(8,128)(2,1)}) %all-gather.3.cloned.1.call-update) | async-done | bytes 9437200 | tf_op jit(solution)/shard_map/all_gather | solution.py:138
  89.4 0.0 copy-done
  89.4 9.0 %expert.1 = bf16[512,2048]{1,0:T(8,128)(2,1)} custom-call(s32[1]{0:T(128)} %bitcast.2.refs_0_, bf16[512,2048]{1,0:T(8,128)(2,1)} %bitcast.18, bf16[16,2,192,768]{3,2,1,0:T(8,128)(2,1)} %bitcast.16), custom_call_target="tpu_custom_call" | custom-call | tf_op jit(solution)/shard_map/expert/pallas_call | solution.py:166
  98.4 57.3 %all_to_all.10 = bf16[16,32,2048]{2,1,0:T(8,128)(2,1)} all-to-all(bf16[16,32,2048]{2,1,0:T(8,128)(2,1)} %bitcast.19), channel_id=1, replica_groups={{0,1,2,3,4,5,6,7,264,265,266,267,268,269,270,271},{16,17,18,19,20,21,22..., dimensions={0} | all-to-all | bytes 4194304 | tf_op jit(solution)/shard_map/all_to_all | solution.py:152
  155.7 3.9 %combine.1 = bf16[128,2048]{1,0:T(8,128)(2,1)} custom-call(bf16[256,512]{1,0:T(8,128)(2,1)} %get-tuple-element.9.refs_0_, bf16[512,2048]{1,0:T(8,128)(2,1)} %bitcast.17), custom_call_target="tpu_custom_call" | custom-call | tf_op jit(solution)/shard_map/combine/pallas_call | solution.py:184
Async XLA Ops:
  6.5 82.8 %all-gather.3.cloned.1.call-start = ((), (), s32[]{:S(2)}) async-start(), calls=%async_computation.2 | async-start | bytes 10027008 | tf_op jit(solution)/shard_map/all_gather | solution.py:138
  7.6 8.1 %collective-permute-start = (bf16[192,768]{1,0:T(8,128)(2,1)S(1)}, bf16[192,768]{1,0:T(8,128)(2,1)S(1)}, u32[]{:S(2)}, u32[]{:S(2)}) collective-permute-start(bf16[192,768]{1,0:T(8,128)(2,1)S(1)} %get-tuple-element.14), channel_id=1, source_target_pairs={{0,256},{16,272},{32,288},{48,304},{64,320},{80,336},{96,352},{112... | collective-permute-start | bytes 884744 | tf_op jit(solution)/shard_map/ppermute | solution.py:126
  16.6 59.5 %all-to-all-start = ((bf16[16,32,2048]{2,1,0:T(8,128)(2,1)}), bf16[16,32,2048]{2,1,0:T(8,128)(2,1)S(1)}, u32[]{:S(2)}, u32[]{:S(2)}) async-start(bf16[16,32,2048]{2,1,0:T(8,128)(2,1)} %bitcast.20), calls=%async_computation | async-start | bytes 4194304 | tf_op jit(solution)/shard_map/all_to_all | solution.py:152
  76.0 13.3 %copy-start = (bf16[16,32,2048]{2,1,0:T(8,128)(2,1)}, bf16[16,32,2048]{2,1,0:T(8,128)(2,1)S(1)}, u32[]{:S(2)}) copy-start(bf16[16,32,2048]{2,1,0:T(8,128)(2,1)S(1)} %all-to-all-done) | copy-start | bytes 6291460
Sparse Core Ops, SparseCore 0:
  16.7 72.5 all-gather.2

commit v8 on v6

--- a/solution.py
+++ b/solution.py
@@ -38,7 +38,7 @@
     factors[count:, :] = (weight - rounded.astype(F32)).astype(BF16)
 
 
-def expert_kernel(side, rows, weights, produced, x, gate, up, down, hidden, out, sems, *, wide, shard):
+def expert_kernel(side, x, weights, produced, gate, up, down, hidden, out, sems, *, wide, shard):
     members = weights.shape[0]
     inner = weights.shape[3]
     features = produced.shape[1]
@@ -62,12 +62,10 @@
             for s in range(2)
         ]
 
-    arrival = begin(rows, x)
     blocks = []
     for first in range(0, inner, wide):
         blocks.append(fetch(0, gate, first, wide) + fetch(1, up, first, wide))
     last = fetch(2, down, 0, inner)
-    arrival.wait()
     for n, first in enumerate(range(0, inner, wide)):
         columns = slice(first, first + wide)
         for copy in blocks[n]:
@@ -139,27 +137,28 @@
             tiled=True,
             axis_index_groups=circles,
         )
-        return moved.reshape(slots, features)
+        return pltpu.with_memory_space_constraint(moved.reshape(slots, features), pltpu.VMEM)
 
     arrived = exchange(outgoing)
     wide = 256
     anywhere = pl.BlockSpec(memory_space=pl.ANY)
+    near = pl.BlockSpec(memory_space=pltpu.VMEM)
     blocks = inner // wide
     anywhere = pl.BlockSpec(memory_space=pl.ANY)
+    near = pl.BlockSpec(memory_space=pltpu.VMEM)
     blocks = inner // wide
     produced = pl.pallas_call(
         lambda *refs: expert_kernel(*refs, wide=wide, shard=shard),
         out_shape=jax.ShapeDtypeStruct((slots, features), BF16),
-        in_specs=[pl.BlockSpec(memory_space=pltpu.SMEM), anywhere, anywhere],
+        in_specs=[pl.BlockSpec(memory_space=pltpu.SMEM), near, anywhere],
         out_specs=anywhere,
         scratch_shapes=[
-            pltpu.VMEM((slots, features), BF16),
             pltpu.VMEM((shards, shard, inner), BF16),
             pltpu.VMEM((shards, shard, inner), BF16),
             pltpu.VMEM((shards, shard, inner), BF16),
             pltpu.VMEM((slots, inner), BF16),
             pltpu.VMEM((slots, features), BF16),
-            pltpu.SemaphoreType.DMA((1 + 4 * blocks + 2 + features // wide,)),
+            pltpu.SemaphoreType.DMA((4 * blocks + 2 + features // wide,)),
         ],
         name="expert",
     )(side, arrived, weights)

time: 166 us -> 165 us (level)
  no operation moved by 1% of the time
where the time goes in v8:
time: 165 us; the launch traced here: 164 us
  waiting for transfers between devices  62.5 us (38%)
  blocking collectives  57.2 us (35%)
  starting transfers between devices  15.1 us (9%)
  Pallas kernels  14.1 us (9%)
  between operations  13.4 us (8%)
  other arithmetic  1.9 us (1%)
    all_to_all x1, blocking collectives, exchange(): lax.all_to_all(blocks, ('dp', 'expert'), split_axis=0, concat_axis=0, til...  57.2 us
    all_to_all x1, waiting for transfers between devices, exchange(): lax.all_to_all(blocks, ('dp', 'expert'), split_axis=0, concat_axis=0, til...  48.3 us
    all_gather x1, waiting for transfers between devices, per_device(): weights = lax.all_gather(both, 'dp', axis=0, axis_index_groups=sides)  13.3 us
    all_to_all x1, starting transfers between devices, exchange(): lax.all_to_all(blocks, ('dp', 'expert'), split_axis=0, concat_axis=0, til...  11.1 us
    pallas_call x1, Pallas kernels, per_device(): pl.pallas_call(lambda *refs: expert_kernel(*refs, wide=wide, shard=shard)...  8.37 us
    ppermute x1, starting transfers between devices, per_device(): other = lax.ppermute(joined, 'dp', swap)  4.02 us
  transfers between devices with their start and end apart: 3, of which 3 were waited for; matrix products, arithmetic and copies ran while one was open for 0% of the time, Pallas kernels for 2%

profile of v8, /device:TPU:1, one launch (start us, length us, event | category | flops | bytes accessed | tf_op | source)
XLA Modules:
  0.0 164.3 jit_solution(12373884184132912767)
XLA Ops:
  6.5 0.0 all-gather.3.cloned.1.call-start
  6.5 1.0 fusion
  7.6 4.0 %collective-permute-start = (bf16[192,768]{1,0:T(8,128)(2,1)S(1)}, bf16[192,768]{1,0:T(8,128)(2,1)S(1)}, u32[]{:S(2)}, u32[]{:S(2)}) collective-permute-start(bf16[192,768]{1,0:T(8,128)(2,1)S(1)} %get-tuple-element.14), channel_id=1, source_target_pairs={{0,256},{16,272},{32,288},{48,304},{64,320},{80,336},{96,352},{112... | collective-permute-start | bytes 884744 | tf_op jit(solution)/shard_map/ppermute | solution.py:106
  11.6 3.3 %dispatch.1 = (bf16[512,2048]{1,0:T(8,128)(2,1)}, bf16[256,512]{1,0:T(8,128)(2,1)}) custom-call(s32[2,128]{1,0:T(2,128)} %bitcast.25, f32[2,128]{1,0:T(2,128)} %bitcast.26, bf16[128,2048]{1,0:T(8,128)(2,1)} %refs_2_.1), custom_call_target="tpu_custom_call" | custom-call | tf_op jit(solution)/shard_map/dispatch/pallas_call | solution.py:107
  14.9 0.8 collective-permute-done
  15.7 0.9 pad_maximum_fusion
  16.6 0.0 all-gather.3.cloned.1.call-update
  16.6 11.1 %all-to-all-start = ((bf16[16,32,2048]{2,1,0:T(8,128)(2,1)}), bf16[16,32,2048]{2,1,0:T(8,128)(2,1)S(1)}, u32[]{:S(2)}, u32[]{:S(2)}) async-start(bf16[16,32,2048]{2,1,0:T(8,128)(2,1)} %bitcast.20), calls=%async_computation | async-start | bytes 4194304 | tf_op jit(solution)/shard_map/all_to_all | solution.py:132
  27.7 48.3 %all-to-all-done = bf16[16,32,2048]{2,1,0:T(8,128)(2,1)S(1)} async-done(((bf16[16,32,2048]{2,1,0:T(8,128)(2,1)}), bf16[16,32,2048]{2,1,0:T(8,128)(2,1)S(1)}, u32[]{:S(2)}, u32[]{:S(2)}) %all-to-all-start) | async-done | bytes 2097184 | tf_op jit(solution)/shard_map/all_to_all | solution.py:132
  76.1 13.3 %all-gather.3.cloned.1.call-done = bf16[32,192,768]{2,1,0:T(8,128)(2,1)} async-done(((bf16[2,192,768]{2,1,0:T(8,128)(2,1)}), bf16[32,192,768]{2,1,0:T(8,128)(2,1)}) %all-gather.3.cloned.1.call-update) | async-done | bytes 9437200 | tf_op jit(solution)/shard_map/all_gather | solution.py:118
  89.4 8.4 %expert.1 = bf16[512,2048]{1,0:T(8,128)(2,1)} custom-call(s32[1]{0:T(128)} %bitcast.2.refs_0_, bf16[512,2048]{1,0:T(8,128)(2,1)S(1)} %bitcast.17, bf16[16,2,192,768]{3,2,1,0:T(8,128)(2,1)} %bitcast.18), custom_call_target="tpu_custom_call" | custom-call | tf_op jit(solution)/shard_map/expert/pallas_call | solution.py:150
  97.7 57.2 %all_to_all.10 = bf16[16,32,2048]{2,1,0:T(8,128)(2,1)S(1)} all-to-all(bf16[16,32,2048]{2,1,0:T(8,128)(2,1)} %bitcast.19), channel_id=1, replica_groups={{0,1,2,3,4,5,6,7,264,265,266,267,268,269,270,271},{16,17,18,19,20,21,22..., dimensions={0} | all-to-all | bytes 4194304 | tf_op jit(solution)/shard_map/all_to_all | solution.py:132
  155.0 2.5 %combine.1 = bf16[128,2048]{1,0:T(8,128)(2,1)} custom-call(bf16[256,512]{1,0:T(8,128)(2,1)} %get-tuple-element.9.factors, bf16[512,2048]{1,0:T(8,128)(2,1)S(1)} %bitcast.16), custom_call_target="tpu_custom_call" | custom-call | tf_op jit(solution)/shard_map/combine/pallas_call | solution.py:166
Async XLA Ops:
  6.5 82.8 %all-gather.3.cloned.1.call-start = ((), (), s32[]{:S(2)}) async-start(), calls=%async_computation.2 | async-start | bytes 10027008 | tf_op jit(solution)/shard_map/all_gather | solution.py:118
  7.6 8.1 %collective-permute-start = (bf16[192,768]{1,0:T(8,128)(2,1)S(1)}, bf16[192,768]{1,0:T(8,128)(2,1)S(1)}, u32[]{:S(2)}, u32[]{:S(2)}) collective-permute-start(bf16[192,768]{1,0:T(8,128)(2,1)S(1)} %get-tuple-element.14), channel_id=1, source_target_pairs={{0,256},{16,272},{32,288},{48,304},{64,320},{80,336},{96,352},{112... | collective-permute-start | bytes 884744 | tf_op jit(solution)/shard_map/ppermute | solution.py:106
  16.6 59.5 %all-to-all-start = ((bf16[16,32,2048]{2,1,0:T(8,128)(2,1)}), bf16[16,32,2048]{2,1,0:T(8,128)(2,1)S(1)}, u32[]{:S(2)}, u32[]{:S(2)}) async-start(bf16[16,32,2048]{2,1,0:T(8,128)(2,1)} %bitcast.20), calls=%async_computation | async-start | bytes 4194304 | tf_op jit(solution)/shard_map/all_to_all | solution.py:132
Sparse Core Ops, SparseCore 0:
  16.7 72.5 all-gather.2

commit v9 on v8

--- a/solution.py
+++ b/solution.py
@@ -167,7 +167,7 @@
         combine_kernel,
         out_shape=jax.ShapeDtypeStruct((count, features), BF16),
         name="combine",
-    )(factors, returned)
+    )(pltpu.with_memory_space_constraint(factors, pltpu.VMEM), returned)
 
 
 def solution(mesh):

time: 165 us -> 164 us (level)
  no operation moved by 1% of the time
where the time goes in v9:
time: 164 us
  waiting for transfers between devices  62.5 us (38%)
  blocking collectives  57.4 us (35%)
  starting transfers between devices  15.1 us (9%)
  between operations  13.4 us (8%)
  Pallas kernels  13.2 us (8%)
  other arithmetic  1.9 us (1%)
    all_to_all x1, blocking collectives, exchange(): lax.all_to_all(blocks, ('dp', 'expert'), split_axis=0, concat_axis=0, til...  57.4 us
    all_to_all x1, waiting for transfers between devices, exchange(): lax.all_to_all(blocks, ('dp', 'expert'), split_axis=0, concat_axis=0, til...  48.3 us
    all_gather x1, waiting for transfers between devices, per_device(): weights = lax.all_gather(both, 'dp', axis=0, axis_index_groups=sides)  13.3 us
    all_to_all x1, starting transfers between devices, exchange(): lax.all_to_all(blocks, ('dp', 'expert'), split_axis=0, concat_axis=0, til...  11.1 us
    pallas_call x1, Pallas kernels, per_device(): pl.pallas_call(lambda *refs: expert_kernel(*refs, wide=wide, shard=shard)...  8.44 us
    ppermute x1, starting transfers between devices, per_device(): other = lax.ppermute(joined, 'dp', swap)  4.02 us
    pallas_call x1, Pallas kernels, per_device(): pl.pallas_call(lambda *refs: dispatch_kernel(*refs, capacity=capacity), o...  3.29 us
  transfers between devices with their start and end apart: 3, of which 3 were waited for; matrix products, arithmetic and copies ran while one was open for 0% of the time, Pallas kernels for 2%

profile of v9, /device:TPU:1, one launch (start us, length us, event | category | flops | bytes accessed | tf_op | source)
XLA Modules:
  0.0 163.6 jit_solution(10194234706953320714)
XLA Ops:
  6.5 0.0 all-gather.3.cloned.1.call-start
  6.5 1.0 fusion
  7.6 4.0 %collective-permute-start = (bf16[192,768]{1,0:T(8,128)(2,1)S(1)}, bf16[192,768]{1,0:T(8,128)(2,1)S(1)}, u32[]{:S(2)}, u32[]{:S(2)}) collective-permute-start(bf16[192,768]{1,0:T(8,128)(2,1)S(1)} %get-tuple-element.14), channel_id=1, source_target_pairs={{0,256},{16,272},{32,288},{48,304},{64,320},{80,336},{96,352},{112... | collective-permute-start | bytes 884744 | tf_op jit(solution)/shard_map/ppermute | solution.py:106
  11.6 3.3 %dispatch.1 = (bf16[512,2048]{1,0:T(8,128)(2,1)}, bf16[256,512]{1,0:T(8,128)(2,1)}) custom-call(s32[2,128]{1,0:T(2,128)} %bitcast.25, f32[2,128]{1,0:T(2,128)} %bitcast.26, bf16[128,2048]{1,0:T(8,128)(2,1)} %refs_2_.1), custom_call_target="tpu_custom_call" | custom-call | tf_op jit(solution)/shard_map/dispatch/pallas_call | solution.py:107
  14.9 0.8 collective-permute-done
  15.7 0.9 pad_maximum_fusion
  16.6 0.0 all-gather.3.cloned.1.call-update
  16.6 11.1 %all-to-all-start = ((bf16[16,32,2048]{2,1,0:T(8,128)(2,1)}), bf16[16,32,2048]{2,1,0:T(8,128)(2,1)S(1)}, u32[]{:S(2)}, u32[]{:S(2)}) async-start(bf16[16,32,2048]{2,1,0:T(8,128)(2,1)} %bitcast.20), calls=%async_computation | async-start | bytes 4194304 | tf_op jit(solution)/shard_map/all_to_all | solution.py:132
  27.7 48.3 %all-to-all-done = bf16[16,32,2048]{2,1,0:T(8,128)(2,1)S(1)} async-done(((bf16[16,32,2048]{2,1,0:T(8,128)(2,1)}), bf16[16,32,2048]{2,1,0:T(8,128)(2,1)S(1)}, u32[]{:S(2)}, u32[]{:S(2)}) %all-to-all-start) | async-done | bytes 2097184 | tf_op jit(solution)/shard_map/all_to_all | solution.py:132
  76.0 13.3 %all-gather.3.cloned.1.call-done = bf16[32,192,768]{2,1,0:T(8,128)(2,1)} async-done(((bf16[2,192,768]{2,1,0:T(8,128)(2,1)}), bf16[32,192,768]{2,1,0:T(8,128)(2,1)}) %all-gather.3.cloned.1.call-update) | async-done | bytes 9437200 | tf_op jit(solution)/shard_map/all_gather | solution.py:118
  89.4 8.4 %expert.1 = bf16[512,2048]{1,0:T(8,128)(2,1)} custom-call(s32[1]{0:T(128)} %bitcast.2.refs_0_, bf16[512,2048]{1,0:T(8,128)(2,1)S(1)} %bitcast.17, bf16[16,2,192,768]{3,2,1,0:T(8,128)(2,1)} %bitcast.18), custom_call_target="tpu_custom_call" | custom-call | tf_op jit(solution)/shard_map/expert/pallas_call | solution.py:150
  97.8 0.0 copy-start
  97.8 57.4 %all_to_all.10 = bf16[16,32,2048]{2,1,0:T(8,128)(2,1)S(1)} all-to-all(bf16[16,32,2048]{2,1,0:T(8,128)(2,1)} %bitcast.19), channel_id=1, replica_groups={{0,1,2,3,4,5,6,7,264,265,266,267,268,269,270,271},{16,17,18,19,20,21,22..., dimensions={0} | all-to-all | bytes 4194304 | tf_op jit(solution)/shard_map/all_to_all | solution.py:132
  155.2 0.0 copy-done
  155.2 1.5 combine.1
Async XLA Ops:
  6.5 82.8 %all-gather.3.cloned.1.call-start = ((), (), s32[]{:S(2)}) async-start(), calls=%async_computation.2 | async-start | bytes 10027008 | tf_op jit(solution)/shard_map/all_gather | solution.py:118
  7.6 8.1 %collective-permute-start = (bf16[192,768]{1,0:T(8,128)(2,1)S(1)}, bf16[192,768]{1,0:T(8,128)(2,1)S(1)}, u32[]{:S(2)}, u32[]{:S(2)}) collective-permute-start(bf16[192,768]{1,0:T(8,128)(2,1)S(1)} %get-tuple-element.14), channel_id=1, source_target_pairs={{0,256},{16,272},{32,288},{48,304},{64,320},{80,336},{96,352},{112... | collective-permute-start | bytes 884744 | tf_op jit(solution)/shard_map/ppermute | solution.py:106
  16.6 59.5 %all-to-all-start = ((bf16[16,32,2048]{2,1,0:T(8,128)(2,1)}), bf16[16,32,2048]{2,1,0:T(8,128)(2,1)S(1)}, u32[]{:S(2)}, u32[]{:S(2)}) async-start(bf16[16,32,2048]{2,1,0:T(8,128)(2,1)} %bitcast.20), calls=%async_computation | async-start | bytes 4194304 | tf_op jit(solution)/shard_map/all_to_all | solution.py:132
  97.8 57.4 %copy-start = (bf16[256,512]{1,0:T(8,128)(2,1)S(1)}, bf16[256,512]{1,0:T(8,128)(2,1)}, u32[]{:S(2)}) copy-start(bf16[256,512]{1,0:T(8,128)(2,1)} %get-tuple-element.9.factors) | copy-start | bytes 786436
Sparse Core Ops, SparseCore 0:
  16.7 72.5 all-gather.2
